TPU v7x, 32 devices: a whole 2x2x4 slice. The times are simulated.
32 devices in a mesh: groups: 2 (over y), ctx: 4 (over x, core), head: 4 (over z).
Axes of the slice: x: 2, y: 2, z: 4, core: 2. Of those that a mesh axis runs over, the one named last changes fastest.
Arguments:
- context: bfloat16 [8192, 1024], P(('groups', 'ctx', 'head')), parts along dimension 0, may hold values from -6 to 6
- w_kv: bfloat16 [1024, 2048], replicated, may hold values from -0.1875 to 0.1875
- queries: bfloat16 [32, 64, 2048], P(('groups', 'head')), parts along dimension 0, may hold values from -400 to 400
- gain: float32 [1024], replicated, may hold values from 0.25 to 1.75
- w_out: bfloat16 [1024, 1024], P('head'), may hold values from -0.1875 to 0.1875
Outputs:
- latent_out: bfloat16 [4096, 1024], P(('groups', 'ctx', 'head')), parts along dimension 0
There are 2 independent parts, one for each index of `groups`. A program takes and returns all parts, laid end to end along the dimension named above; an argument that names none is the same for every part. Nothing has to cross between parts.
All inputs are finite; a program needn't handle non-finite values.
Results may differ from a plain program's by a relative error of at most 0.01575.
Values may be sent and summed in bfloat16 or wider, within the bound.
No kernel may reach another device: no remote copies, remote signals or barrier semaphores. Data moves between devices by JAX's collectives and lax.ppermute only.
A program may use at most 64 MiB of HBM per device.

v0:
```python
import math

import jax
import jax.numpy as jnp
from jax import lax
from jax.sharding import PartitionSpec as P

epsilon = 1e-06


def body(context, w_kv, queries, gain, w_out):
    heads_local, head_size, latents = queries.shape
    model_width = w_kv.shape[0]
    total_heads = w_kv.shape[1] // (2 * head_size)
    head_count = lax.axis_size("head")
    ctx_count = lax.axis_size("ctx")
    head_scale = 1.0 / math.sqrt(head_size)
    projected = jnp.dot(context, w_kv, preferred_element_type=jnp.float32).astype(jnp.bfloat16)
    projected = projected.reshape(context.shape[0], total_heads, 2 * head_size)
    regrouped = lax.all_to_all(projected, "head", split_axis=1, concat_axis=0, tiled=True)
    key_rows = regrouped[:, :, :head_size]
    value_rows = regrouped[:, :, head_size:]
    block_size = min(512, latents)
    block_count = latents // block_size
    query_blocks = queries.reshape(heads_local, head_size, block_count, block_size)

    def attend(position):
        query_block = lax.dynamic_index_in_dim(query_blocks, position, 2, keepdims=False)
        scores = (
            jnp.einsum("hdq,khd->hqk", query_block, key_rows, preferred_element_type=jnp.float32)
            * head_scale
        )
        highest = jnp.max(scores, axis=2)
        weights = jnp.exp(scores - highest[:, :, None])
        row_total = jnp.sum(weights, axis=2)
        summed = jnp.einsum(
            "hqk,khd->hqd",
            weights.astype(jnp.bfloat16),
            value_rows,
            preferred_element_type=jnp.float32,
        )
        return (highest, row_total, summed)

    maxima, totals, partials = lax.map(attend, jnp.arange(block_count))
    maxima = maxima.transpose(1, 0, 2).reshape(heads_local, latents)
    totals = totals.transpose(1, 0, 2).reshape(heads_local, latents)
    partials = partials.transpose(1, 0, 2, 3).reshape(heads_local, latents * head_size // 128, 128)
    ctx_rows = latents // ctx_count
    overall = lax.pmax(maxima, "ctx")
    factor = jnp.exp(maxima - overall)
    spread = partials.reshape(heads_local, latents, head_size) * factor[:, :, None]
    scaled = spread.reshape(heads_local, latents * head_size // 128, 128)
    sums_own, total_own = (
        lax.psum_scatter(
            scaled.astype(jnp.bfloat16), "ctx", scatter_dimension=1, tiled=True
        ).astype(jnp.float32),
        lax.psum_scatter(
            (totals * factor).astype(jnp.bfloat16), "ctx", scatter_dimension=1, tiled=True
        ).astype(jnp.float32),
    )
    sums_own = sums_own.reshape(heads_local, ctx_rows, head_size)
    attended = sums_own / total_own[:, :, None]
    own_rows = ctx_rows // head_count
    packed = attended.reshape(heads_local, head_count, own_rows * head_size)
    gathered = lax.all_to_all(
        packed.astype(jnp.bfloat16), "head", split_axis=1, concat_axis=0, tiled=True
    ).astype(packed.dtype)
    joined = (
        gathered.reshape(total_heads, own_rows, head_size)
        .transpose(1, 0, 2)
        .reshape(own_rows, model_width)
    )
    mean_square = jnp.sum(joined * joined, axis=1, keepdims=True) / model_width
    normed = (joined * gain[None, :] * lax.rsqrt(mean_square + epsilon)).astype(jnp.bfloat16)
    result = jnp.dot(
        normed,
        lax.all_gather(w_out, "head", axis=0, tiled=True),
        preferred_element_type=jnp.float32,
    )
    return result.astype(jnp.bfloat16)


def solution(mesh):
    return jax.shard_map(
        body,
        mesh=mesh,
        in_specs=(
            P(("groups", "ctx", "head"), None),
            P(),
            P(("groups", "head"), None, None),
            P(),
            P("head", None),
        ),
        out_specs=P(("groups", "ctx", "head"), None),
        check_vma=False,
    )
```

profile of v0, /device:TPU:0, one launch (start us, length us, event | category | flops | bytes accessed | tf_op | source)
XLA Modules:
  0.0 184.5 jit_solution(581980694861545381)
XLA Ops:
  7.4 0.0 copy-start
  7.4 1.0 copy-done
  8.4 3.4 %fusion.15 = bf16[32,16,8,128]{3,2,1,0:T(8,128)(2,1)S(1)} fusion(bf16[256,1024]{1,0:T(8,128)(2,1)S(1)} %copy-done, bf16[1024,2048]{1,0:T(8,128)(2,1)} %param.8), kind=kOutput, calls=%fused_computation.16 | convolution fusion | flops 1074266112 | bytes 5767168 | tf_op jit(solution)/shard_map/dot_general | solution.py:18
  11.9 1.3 copy.24
  13.1 6.3 %all-to-all-start = ((bf16[256,16,128]{2,0,1:T(8,128)(2,1)}), bf16[256,16,128]{2,0,1:T(8,128)(2,1)S(1)}, u32[]{:S(2)}, u32[]{:S(2)}) async-start(bf16[256,16,128]{2,0,1:T(8,128)(2,1)} %bitcast.58), calls=%async_computation | async-start | bytes 2097152 | tf_op jit(solution)/shard_map/all_to_all | solution.py:20
  19.5 0.0 reduce-scatter.7.cloned.1.call-start
  19.5 1.3 copy.25
  20.8 24.4 %all-to-all-done = bf16[256,16,128]{2,0,1:T(8,128)(2,1)S(1)} async-done(((bf16[256,16,128]{2,0,1:T(8,128)(2,1)}), bf16[256,16,128]{2,0,1:T(8,128)(2,1)S(1)}, u32[]{:S(2)}, u32[]{:S(2)}) %all-to-all-start) | async-done | bytes 1048608 | tf_op jit(solution)/shard_map/all_to_all | solution.py:20
  45.2 1.5 copy.13
  46.7 2.6 %all_to_all.23 = bf16[1024,4,128]{0,2,1:T(8,128)(2,1)} reshape(bf16[4,256,4,128]{1,0,3,2:T(4,128)(2,1)} %copy.13) | data formatting | bytes 2097152 | tf_op jit(solution)/shard_map/all_to_all | solution.py:20
  49.2 1.3 fusion.18
  50.5 32.3 %while.14 = (s32[]{:T(128)}, f32[4,4,512]{2,1,0:T(4,128)S(1)}, f32[4,4,512]{2,1,0:T(4,128)S(1)}, f32[4,4,512,64]{2,3,1,0:T(8,128)}, s32[4]{0:T(128)S(1)}, /*inde...) while((s32[]{:T(128)}, f32[4,4,512]{2,1,0:T(4,128)S(1)}, ...), condition=%wide.region_3.4_spmd, body=%wide.region_0.3_spmd.sunk | while | flops 553644032 | bytes 27067044 | solution.py:44
  50.5 0.6 dynamic_slice.17
  52.8 1.4 multiply_reduce_fusion.3
  54.2 2.6 %fusion.34 = f32[4,4,512,64]{2,3,1,0:T(8,128)} fusion(f32[4,4,512,64]{2,3,1,0:T(8,128)} %get-tuple-element.163, s32[]{:T(128)} %get-tuple-element.160, bf16[1024,4,64]{0,2,1:T(8,128)(2,1)S(1)} %get-tuple-element.178, f32[4,512,1024]{2,1,0:T(8,128)S(1)} %get-tuple-element.145, f32[4,512]{1,0:T(4,128)S(1)} %get-tuple-element.146), kind=kOutput, calls=%fused_computation.6.clone.1 | convolution fusion | flops 274726912 | bytes 9445888 | tf_op jit(solution)/shard_map/while/body/eval_jaxpr/hqk,khd->hqd/dot_general | solution.py:36
  56.8 1.8 fusion.33
  58.6 0.6 dynamic_slice.17
  60.9 1.4 multiply_reduce_fusion.3
  62.3 2.6 %fusion.34 = f32[4,4,512,64]{2,3,1,0:T(8,128)} fusion(f32[4,4,512,64]{2,3,1,0:T(8,128)} %get-tuple-element.163, s32[]{:T(128)} %get-tuple-element.160, bf16[1024,4,64]{0,2,1:T(8,128)(2,1)S(1)} %get-tuple-element.178, f32[4,512,1024]{2,1,0:T(8,128)S(1)} %get-tuple-element.145, f32[4,512]{1,0:T(4,128)S(1)} %get-tuple-element.146), kind=kOutput, calls=%fused_computation.6.clone.1 | convolution fusion | flops 274726912 | bytes 9445888 | tf_op jit(solution)/shard_map/while/body/eval_jaxpr/hqk,khd->hqd/dot_general | solution.py:36
  64.9 1.8 fusion.33
  66.7 0.6 dynamic_slice.17
  69.0 1.4 multiply_reduce_fusion.3
  70.4 2.6 %fusion.34 = f32[4,4,512,64]{2,3,1,0:T(8,128)} fusion(f32[4,4,512,64]{2,3,1,0:T(8,128)} %get-tuple-element.163, s32[]{:T(128)} %get-tuple-element.160, bf16[1024,4,64]{0,2,1:T(8,128)(2,1)S(1)} %get-tuple-element.178, f32[4,512,1024]{2,1,0:T(8,128)S(1)} %get-tuple-element.145, f32[4,512]{1,0:T(4,128)S(1)} %get-tuple-element.146), kind=kOutput, calls=%fused_computation.6.clone.1 | convolution fusion | flops 274726912 | bytes 9445888 | tf_op jit(solution)/shard_map/while/body/eval_jaxpr/hqk,khd->hqd/dot_general | solution.py:36
  72.9 1.8 fusion.33
  74.8 0.6 dynamic_slice.17
  77.0 1.4 multiply_reduce_fusion.3
  78.4 2.6 %fusion.34 = f32[4,4,512,64]{2,3,1,0:T(8,128)} fusion(f32[4,4,512,64]{2,3,1,0:T(8,128)} %get-tuple-element.163, s32[]{:T(128)} %get-tuple-element.160, bf16[1024,4,64]{0,2,1:T(8,128)(2,1)S(1)} %get-tuple-element.178, f32[4,512,1024]{2,1,0:T(8,128)S(1)} %get-tuple-element.145, f32[4,512]{1,0:T(4,128)S(1)} %get-tuple-element.146), kind=kOutput, calls=%fused_computation.6.clone.1 | convolution fusion | flops 274726912 | bytes 9445888 | tf_op jit(solution)/shard_map/while/body/eval_jaxpr/hqk,khd->hqd/dot_general | solution.py:36
  81.0 1.8 fusion.33
  82.8 10.4 %pmax.7 = f32[4,2048]{1,0:T(4,128)S(1)} all-reduce(f32[4,2048]{1,0:T(4,128)S(1)} %bitcast.79), channel_id=1, replica_groups=mesh['groups'=2,'ctx'=4,'head'=4] {'ctx'}, use_global_device_ids=true, to_apply=%region_4.5 | all-reduce | flops 8192 | bytes 65536 | tf_op jit(solution)/shard_map/pmax | solution.py:49
  93.2 2.6 %mul.37 = f32[4,2048,64]{2,1,0:T(8,128)} broadcast(f32[4,2048]{1,0:T(4,128)S(1)} %get-tuple-element.85), dimensions={0,1} | broadcast | bytes 2129920 | tf_op jit(solution)/shard_map/mul | solution.py:51
  95.8 4.6 %mul.38 = f32[4,1024,128]{2,1,0:T(8,128)} reshape(f32[4,2048,64]{2,1,0:T(8,128)} %mul.37) | data formatting | bytes 4194304 | tf_op jit(solution)/shard_map/mul | solution.py:51
  100.5 3.8 %copy.15 = f32[4,4,512,64]{3,2,1,0:T(8,128)} copy(f32[4,4,512,64]{2,3,0,1:T(8,128)} %bitcast.75) | data formatting | bytes 4194304 | tf_op jit(solution)/shard_map/transpose | solution.py:47
  104.2 4.6 %reshape_reshape.3 = f32[4,1024,128]{2,1,0:T(8,128)} reshape(f32[4,4,512,64]{3,2,1,0:T(8,128)} %copy.15) | data formatting | bytes 4194304 | tf_op jit(solution)/shard_map/reshape;reshape | solution.py:51
  108.9 1.1 copy.18
  109.9 0.0 reduce-scatter.7.cloned.1.call-update
  109.9 0.0 reduce-scatter.5.cloned.1.call-start
  110.0 3.4 %multiply_convert_fusion = bf16[4,1024,128]{2,1,0:T(8,128)(2,1)} fusion(f32[4,1024,128]{2,1,0:T(8,128)} %reshape_reshape.3, f32[4,1024,128]{2,1,0:T(8,128)} %mul.38), kind=kLoop, calls=%fused_computation.15 | loop fusion | flops 1048576 | bytes 5242880 | tf_op jit(solution)/shard_map/convert_element_type | solution.py:55
  113.4 0.0 reduce-scatter.5.cloned.1.call-update
  113.5 0.0 all-gather.2.cloned.1.call-start
  113.5 0.5 all-gather.2.cloned.1.call-update
  114.0 16.9 %reduce-scatter.7.cloned.1.call-done = bf16[512,4]{1,0:T(8,128)(2,1)} async-done(((bf16[2048,4]{1,0:T(8,128)(2,1)}), bf16[512,4]{1,0:T(8,128)(2,1)}) %reduce-scatter.7.cloned.1.call-update) | async-done | bytes 4112
  130.9 1.0 copy.19
  131.9 0.3 div.17
  132.3 0.4 div.18
  132.7 0.0 copy-start.1
  132.7 25.6 %reduce-scatter.5.cloned.1.call-done = bf16[4,256,128]{2,1,0:T(8,128)(2,1)} async-done(((bf16[4,1024,128]{2,1,0:T(8,128)(2,1)}), bf16[4,256,128]{2,1,0:T(8,128)(2,1)}) %reduce-scatter.5.cloned.1.call-update) | async-done | bytes 262160 | tf_op jit(solution)/shard_map/reduce_scatter | solution.py:54
  158.3 1.2 reshape.56
  159.4 0.1 divide_convert_fusion
  159.6 0.2 copy.16
  159.8 13.1 %all_to_all.27 = bf16[4,4,8192]{2,0,1:T(4,128)(2,1)S(1)} all-to-all(bf16[4,4,8192]{2,0,1:T(4,128)(2,1)S(1)} %copy.16), channel_id=1, replica_groups=mesh['groups'=2,'ctx'=4,'head'=4] {'head'}, dimensions={1} | all-to-all | bytes 524288 | tf_op jit(solution)/shard_map/all_to_all | solution.py:65
  172.9 0.5 reshape.57
  173.5 0.3 copy.17
  173.8 0.2 multiply_reduce_fusion.1
  174.0 0.0 copy-done.1
  174.0 0.2 fusion.17
  174.2 0.0 all-gather.2.cloned.1.call-done
  174.3 2.8 %convolution_convert_fusion.1 = bf16[128,1024]{1,0:T(8,128)(2,1)} fusion(bf16[128,1024]{0,1:T(8,128)(2,1)S(1)} %fusion.17, bf16[1024,1024]{1,0:T(8,128)(2,1)} %all-gather.2.cloned.1.call-done), kind=kOutput, calls=%fused_computation.17 | convolution fusion | flops 268566528 | bytes 2621440 | tf_op jit(solution)/shard_map/dot_general | solution.py:75
  (11 shorter events, 0.1 us)
Async XLA Ops:
  7.4 1.0 copy-start
  13.1 32.1 %all-to-all-start = ((bf16[256,16,128]{2,0,1:T(8,128)(2,1)}), bf16[256,16,128]{2,0,1:T(8,128)(2,1)S(1)}, u32[]{:S(2)}, u32[]{:S(2)}) async-start(bf16[256,16,128]{2,0,1:T(8,128)(2,1)} %bitcast.58), calls=%async_computation | async-start | bytes 2097152 | tf_op jit(solution)/shard_map/all_to_all | solution.py:20
  19.5 111.4 %reduce-scatter.7.cloned.1.call-start = ((), (), s32[]{:S(2)}) async-start(), calls=%async_computation.6 | async-start | bytes 655360
  109.9 48.3 %reduce-scatter.5.cloned.1.call-start = ((), (), s32[]{:S(2)}) async-start(), calls=%async_computation.4 | async-start | bytes 1310720 | tf_op jit(solution)/shard_map/reduce_scatter | solution.py:54
  113.5 60.8 %all-gather.2.cloned.1.call-start = ((), (), s32[]{:S(2)}) async-start(), calls=%async_computation.5 | async-start | bytes 2621440 | tf_op jit(solution)/shard_map/all_gather | solution.py:77
  132.7 41.3 %copy-start.1 = (f32[1024]{0:T(1024)S(1)}, f32[1024]{0:T(1024)}, u32[]{:S(2)}) copy-start(f32[1024]{0:T(1024)} %param.10) | copy-start | bytes 12292
Sparse Core Ops, SparseCore 0:
  110.1 20.8 reduce-scatter.6
  133.4 24.7 reduce-scatter.4
Sparse Core Ops, SparseCore 1:
  115.5 44.6 all-gather.1
where the time goes:
time: 185 us; the launch traced here: 184 us
  waiting for transfers between devices  67.4 us (36%)
  local copies, waits for them, and re-layouts  32 us (17%)
  blocking collectives  23.5 us (13%)
  matrix products  22.1 us (12%)
  between operations  15 us (8%)
  other arithmetic  11.3 us (6%)
  loops' own time  6.81 us (4%)
  starting transfers between devices  6.43 us (3%)
    reduce_scatter x1, waiting for transfers between devices, body(): lax.psum_scatter(scaled.astype(jnp.bfloat16), 'ctx', scatter_dimension=1,...  25.6 us
    all_to_all x1, waiting for transfers between devices, body(): lax.all_to_all(projected, 'head', split_axis=1, concat_axis=0, tiled=True)  24.4 us
    unnamed x4, waiting for transfers between devices  17.4 us
    all_to_all x1, blocking collectives, body(): lax.all_to_all(packed.astype(jnp.bfloat16), 'head', split_axis=1, concat_...  13.1 us
    pmax x1, blocking collectives, body(): overall = lax.pmax(maxima, 'ctx')  10.4 us
    dot_general x4, matrix products, attend(): jnp.einsum('hqk,khd->hqd', weights.astype(jnp.bfloat16), value_rows, pref...  10.3 us
    mul x2, local copies, waits for them, and re-layouts, body(): partials.reshape(heads_local, latents, head_size) * factor[:, :, None]  7.21 us
    reduce_sum x4, other arithmetic, attend(): row_total = jnp.sum(weights, axis=2)  7.21 us
  transfers between devices with their start and end apart: 4, of which 3 were waited for; matrix products, arithmetic and copies ran while one was open for 5% of the time, Pallas kernels for 0%

commit v1 on v0

--- a/solution.py
+++ b/solution.py
@@ -1,14 +1,380 @@
+import functools
 import math
 
 import jax
 import jax.numpy as jnp
 from jax import lax
+from jax.experimental import pallas as pl
+from jax.experimental.pallas import tpu as pltpu
 from jax.sharding import PartitionSpec as P
 
+
 epsilon = 1e-06
-
-
-def body(context, w_kv, queries, gain, w_out):
+stat_rows = 8
+f32 = jnp.float32
+bf16 = jnp.bfloat16
+
+vmem = pl.BlockSpec(memory_space=pltpu.VMEM)
+in_hbm = pl.BlockSpec(memory_space=pltpu.HBM)
+
+
+def call(kernel, out_shape, args, flops=0, transcendentals=0, scratch=(), in_specs=None):
+    moved = sum(math.prod(a.shape) * a.dtype.itemsize for a in args)
+    return pl.pallas_call(
+        kernel,
+        out_shape=out_shape,
+        in_specs=in_specs or [vmem] * len(args),
+        out_specs=[vmem] * len(out_shape),
+        scratch_shapes=list(scratch),
+        compiler_params=pltpu.CompilerParams(vmem_limit_bytes=24 << 20),
+        cost_estimate=pl.CostEstimate(
+            flops=int(flops), transcendentals=int(transcendentals), bytes_accessed=int(moved)
+        ),
+    )(*args)
+
+
+def shape(dims, dtype):
+    return jax.ShapeDtypeStruct(tuple(dims), dtype)
+
+
+def partner(value, axis, step):
+    count = lax.axis_size(axis)
+    return lax.ppermute(value, axis, [(i, i ^ step) for i in range(count)])
+
+
+def project_kernel(total, offset, width, size, scale, piece, x_ref, w_ref, *rest):
+    count = lax.axis_size("head")
+    carried_ref, rest = (rest[0], rest[1:]) if piece else (None, rest)
+    outs, slots, sems = rest[:count], rest[count], rest[count + 1]
+    rows = x_ref.shape[0]
+    here = lax.axis_index("head")
+    copies = []
+    order = list(range(count - 1, -1, -1))
+    for step in order:
+        first = (here ^ step) * total + offset
+        columns = pl.ds(pl.multiple_of(first, 128), width)
+        copy = pltpu.make_async_copy(w_ref.at[:, columns], slots.at[step], sems.at[step])
+        copy.start()
+        copies.append(copy)
+    column = lax.broadcasted_iota(jnp.int32, (1, width), 1)
+    factor = jnp.where(lax.rem(column, 2 * size) < size, scale, 1.0).astype(f32)
+    if piece:
+        place = lax.axis_index("groups") * lax.axis_size("ctx") + lax.axis_index("ctx")
+        own = carried_ref[pl.ds(pl.multiple_of(place * piece, piece), piece), :]
+    for copy, step in zip(copies, order):
+        copy.wait()
+        product = jnp.dot(x_ref[...], slots[step], preferred_element_type=f32)
+        outs[step][0:rows, :] = (product * factor).astype(bf16)
+        if piece:
+            for j, at in enumerate(range(0, own.shape[1], width)):
+                part = own[:, at : at + width]
+                outs[step][rows + j * piece : rows + (j + 1) * piece, 0 : part.shape[1]] = part
+
+
+def project(context, w_kv, w_out, offset, heads, size, pieces):
+    count = lax.axis_size("head")
+    rows, depth = context.shape
+    width = 2 * size * heads
+    total = w_kv.shape[1] // count
+    piece = w_out.shape[0] // pieces if w_out is not None else 0
+    extra = piece * (-(-w_out.shape[1] // width)) if piece else 0
+    args = [context, w_kv] + ([w_out] if piece else [])
+    return call(
+        functools.partial(
+            project_kernel, total, 2 * size * offset, width, size, 1.0 / math.sqrt(size), piece
+        ),
+        [shape((rows + extra, width), bf16)] * count,
+        args,
+        flops=2 * rows * depth * width * count,
+        scratch=[pltpu.VMEM((count, depth, width), bf16), pltpu.SemaphoreType.DMA((count,))],
+        in_specs=[vmem, in_hbm] + ([vmem] if piece else []),
+    )
+
+
+def split_stats(top, total):
+    rows = []
+    for value in (top, total):
+        for _ in range(3):
+            part = value.astype(bf16).astype(f32)
+            rows.append(part)
+            value = value - part
+    pad = jnp.zeros((stat_rows - len(rows), top.shape[1]), f32)
+    return jnp.concatenate(rows + [pad], axis=0).astype(bf16)
+
+
+def join_stats(block):
+    rows = block.astype(f32)
+    return rows[0:1] + rows[1:2] + rows[2:3], rows[3:4] + rows[4:5] + rows[5:6]
+
+
+def attend_kernel(offset, rows, sources, tile, first, last, q_ref, *rest):
+    kv_refs, rest = rest[:sources], rest[sources:]
+    if not first:
+        (old_ref, old_stat_ref), rest = rest[:2], rest[2:]
+    outs, scores_ref = rest[:-1], rest[-1]
+    _, size, latents = q_ref.shape
+    heads = kv_refs[0].shape[1] // (2 * size)
+    blocks = lax.axis_size("ctx")
+    block = latents // blocks
+    parity = lax.axis_index("ctx") & 1
+    parts = block // tile
+    work = [
+        (head, pair, which, part)
+        for head in range(heads)
+        for which in range(2)
+        for pair in range(blocks // 2)
+        for part in range(parts)
+    ]
+    keys, values = {}, {}
+
+    def lanes_of(item):
+        _, pair, which, part = item
+        if not last:
+            return pl.ds((2 * pair + which) * block + part * tile, tile)
+        which = parity if which else 1 - parity
+        start = (2 * pair + which) * block + part * tile
+        return pl.ds(pl.multiple_of(start, 128), tile)
+
+    def scores(item, slot):
+        head = item[0]
+        if head not in keys:
+            at = 2 * head * size
+            keys[head] = [r[0:rows, at : at + size] for r in kv_refs]
+            values[head] = [
+                r[0:rows, at + size : at + 2 * size].astype(f32).T.astype(bf16) for r in kv_refs
+            ]
+        query = q_ref[offset + head, :, lanes_of(item)]
+        top = None if first else old_stat_ref[head, 0:1, lanes_of(item)]
+        for i in range(sources):
+            s = jnp.dot(keys[head][i], query, preferred_element_type=f32)
+            scores_ref[slot, i] = s
+            peak = jnp.max(s, axis=0, keepdims=True)
+            top = peak if top is None else jnp.maximum(top, peak)
+        return top
+
+    def finish(item, slot, top):
+        head, pair, which, part = item
+        lanes = lanes_of(item)
+        if first:
+            total, summed = 0.0, 0.0
+        else:
+            fade = jnp.exp(old_stat_ref[head, 0:1, lanes] - top)
+            total = old_stat_ref[head, 1:2, lanes] * fade
+            summed = old_ref[head, :, lanes] * fade
+        for i in range(sources):
+            weights = jnp.exp(scores_ref[slot, i] - top)
+            total += jnp.sum(weights, axis=0, keepdims=True)
+            summed += jnp.dot(values[head][i], weights.astype(bf16), preferred_element_type=f32)
+        if not last:
+            outs[0][head, :, lanes] = summed
+            outs[1][head, 0:1, lanes] = top
+            outs[1][head, 1:2, lanes] = total
+            return
+        at = pl.ds(pair * block + part * tile, tile)
+        if which == 0:
+            outs[0][head, 0:size, at] = summed.astype(bf16)
+            outs[0][head, size:, at] = split_stats(top, total)
+        else:
+            outs[1][head, :, at] = summed
+            outs[2][head, 0:1, at] = top
+            outs[2][head, 1:2, at] = total
+
+    top = scores(work[0], 0)
+    for n, item in enumerate(work):
+        later = scores(work[n + 1], (n + 1) % 2) if n + 1 < len(work) else None
+        finish(item, n % 2, top)
+        top = later
+
+
+def attend(queries, parts, state, rows, offset, last):
+    _, size, latents = queries.shape
+    heads = parts[0].shape[1] // (2 * size)
+    tile = min(512, latents // lax.axis_size("ctx"))
+    work = heads * latents * rows * len(parts)
+    half = latents // 2
+    if last:
+        out_shape = [
+            shape((heads, size + stat_rows, half), bf16),
+            shape((heads, size, half), f32),
+            shape((heads, 2, half), f32),
+        ]
+    else:
+        out_shape = [shape((heads, size, latents), f32), shape((heads, 2, latents), f32)]
+    return call(
+        functools.partial(attend_kernel, offset, rows, len(parts), tile, state is None, last),
+        out_shape,
+        [queries, *parts, *(state or ())],
+        flops=4 * work * size,
+        transcendentals=work,
+        scratch=[pltpu.VMEM((2, len(parts), rows, tile), f32)],
+    )
+
+
+def merge_kernel(level, last, got_ref, keep_ref, stat_ref, *outs):
+    heads, size, lanes = keep_ref.shape
+    count = lax.axis_size("ctx") >> level
+    others = lax.axis_size("head")
+    here = lax.axis_index("head")
+    for head in range(heads):
+
+        def merged(at):
+            m_got, t_got = join_stats(got_ref[head, size:, at])
+            m_own, t_own = stat_ref[head, 0:1, at], stat_ref[head, 1:2, at]
+            top = jnp.maximum(m_got, m_own)
+            f_got, f_own = jnp.exp(m_got - top), jnp.exp(m_own - top)
+            total = t_got * f_got + t_own * f_own
+            summed = got_ref[head, 0:size, at].astype(f32) * f_got + keep_ref[head, :, at] * f_own
+            return summed, top, total
+
+        if last:
+            own = lanes // others
+            for step in range(others):
+                at = pl.ds(pl.multiple_of((here ^ step) * own, 128), own)
+                summed, _, total = merged(at)
+                outs[step][head] = (summed / total).astype(bf16)
+            continue
+        send_ref, next_ref, next_stat_ref = outs
+        width = lanes // count
+        parity = (lax.axis_index("ctx") >> level) & 1
+        for pair in range(count // 2):
+            to = slice(pair * width, (pair + 1) * width)
+            at = pl.ds(pl.multiple_of((2 * pair + 1 - parity) * width, 128), width)
+            summed, top, total = merged(at)
+            send_ref[head, 0:size, to] = summed.astype(bf16)
+            send_ref[head, size:, to] = split_stats(top, total)
+            at = pl.ds(pl.multiple_of((2 * pair + parity) * width, 128), width)
+            summed, top, total = merged(at)
+            next_ref[head, :, to] = summed
+            next_stat_ref[head, 0:1, to] = top
+            next_stat_ref[head, 1:2, to] = total
+
+
+def merge(level, got, keep, stat):
+    heads, size, lanes = keep.shape
+    last = (lax.axis_size("ctx") >> level) == 1
+    if last:
+        others = lax.axis_size("head")
+        out_shape = [shape((heads, size, lanes // others), bf16)] * others
+    else:
+        out_shape = [
+            shape((heads, size + stat_rows, lanes // 2), bf16),
+            shape((heads, size, lanes // 2), f32),
+            shape((heads, 2, lanes // 2), f32),
+        ]
+    return call(
+        functools.partial(merge_kernel, level, last),
+        out_shape,
+        [got, keep, stat],
+        flops=4 * heads * size * lanes,
+    )
+
+
+def unpack_kernel(rows, piece, *refs):
+    out_ref = refs[-1]
+    columns = out_ref.shape[2]
+    for step, ref in enumerate(refs[:-1]):
+        width = ref.shape[1]
+        for j, at in enumerate(range(0, columns, width)):
+            wide = min(width, columns - at)
+            out_ref[step, :, at : at + wide] = ref[
+                rows + j * piece : rows + (j + 1) * piece, 0:wide
+            ]
+
+
+def pair_kernel(a_ref, b_ref, out_ref):
+    out_ref[0 : a_ref.shape[0]] = a_ref[...]
+    out_ref[a_ref.shape[0] :] = b_ref[...]
+
+
+def order_kernel(offsets, *refs):
+    out_ref = refs[-1]
+    place = lax.axis_index("groups") * lax.axis_size("ctx") + lax.axis_index("ctx")
+    j = 0
+    for ref in refs[:-1]:
+        piece = ref.shape[2]
+        for i in range(ref.shape[0]):
+            start = pl.multiple_of((place ^ offsets[j]) * piece, piece)
+            out_ref[:, pl.ds(start, piece), :] = ref[i]
+            j += 1
+
+
+def gather_w_out(parts, rows, w_out, pieces):
+    heads, columns = len(parts), w_out.shape[1]
+    piece = w_out.shape[0] // pieces
+    (held,) = call(
+        functools.partial(unpack_kernel, rows, piece), [shape((heads, piece, columns), bf16)], parts
+    )
+    held = held.reshape(1, heads, piece, columns)
+    ctx = lax.axis_size("ctx")
+    steps = [("ctx", 1 << b, 1 << b) for b in range(1, (ctx - 1).bit_length())]
+    steps += [
+        ("groups", 1 << b, ctx << b) for b in range((lax.axis_size("groups") - 1).bit_length())
+    ]
+    offsets = [0]
+    groups = [held]
+    for n, (axis, bit, weight) in enumerate(steps):
+        got = partner(held, axis, bit)
+        offsets = offsets + [o ^ weight for o in offsets]
+        if n + 1 < len(steps):
+            (held,) = call(
+                pair_kernel, [shape((2 * held.shape[0],) + held.shape[1:], bf16)], [held, got]
+            )
+            groups = [held]
+        else:
+            groups = [held, got]
+    groups = groups + [partner(g, "ctx", 1) for g in groups]
+    offsets = offsets + [o ^ 1 for o in offsets]
+    (full,) = call(
+        functools.partial(order_kernel, offsets),
+        [shape((heads, w_out.shape[0], columns), bf16)],
+        groups,
+    )
+    return full
+
+
+def output_kernel(chunk_heads, x_count, *refs):
+    out_ref = refs[-1]
+    gain_ref, w_ref = refs[x_count], refs[x_count + 1]
+    count = lax.axis_size("head")
+    here = lax.axis_index("head")
+    size = refs[0].shape[1]
+    own = refs[0].shape[2]
+    width = w_ref.shape[0] * w_ref.shape[1]
+    blocks = []
+    square = jnp.zeros((1, own), f32)
+    for step in range(count):
+        start = 0
+        for n, heads in enumerate(chunk_heads):
+            block = refs[n * count + step][...].reshape(heads * size, own).astype(f32)
+            square += jnp.sum(block * block, axis=0, keepdims=True)
+            blocks.append((step, start * size, heads * size, block))
+            start += heads
+    factor = lax.rsqrt(square / width + epsilon)
+    factor = jnp.broadcast_to(factor, (128, own)).T[:, 0:1]
+    result = jnp.zeros((own, w_ref.shape[2]), f32)
+    for step, start, rows, block in blocks:
+        gain = gain_ref[here ^ step, :, start : start + rows]
+        normed = (block.T * gain * factor).astype(bf16)
+        result += jnp.dot(
+            normed, w_ref[step, start : start + rows, :], preferred_element_type=f32
+        )
+    out_ref[...] = result.astype(bf16)
+
+
+def output(pieces, chunk_heads, gain, w_full):
+    count, rows, columns = w_full.shape
+    args = [p for chunk in pieces for p in chunk]
+    own = args[0].shape[2]
+    (result,) = call(
+        functools.partial(output_kernel, chunk_heads, len(args)),
+        [shape((own, columns), bf16)],
+        args + [gain.reshape(count, 1, rows), w_full],
+        flops=2 * own * count * rows * columns,
+    )
+    return result
+
+
+def plain_body(context, w_kv, queries, gain, w_out):
     heads_local, head_size, latents = queries.shape
     model_width = w_kv.shape[0]
     total_heads = w_kv.shape[1] // (2 * head_size)
@@ -80,6 +446,66 @@
     return result.astype(jnp.bfloat16)
 
 
+def fast_shapes(context, queries, w_out):
+    heads_local, size, latents = queries.shape
+    head_count, ctx_count = lax.axis_size("head"), lax.axis_size("ctx")
+    pieces = ctx_count * lax.axis_size("groups")
+    powers = (head_count, ctx_count, pieces, size)
+    return (
+        all(n > 0 and n & (n - 1) == 0 for n in powers)
+        and (size.bit_length() - 1) % 2 == 0
+        and size % 16 == 0
+        and ctx_count > 1
+        and head_count > 1
+        and heads_local == sum(CHUNKS)
+        and (latents // (ctx_count * head_count)) % 128 == 0
+        and latents // ctx_count <= 512
+        and context.shape[0] % 16 == 0
+        and (w_out.shape[0] // pieces) % 16 == 0
+    )
+
+
+def body(context, w_kv, queries, gain, w_out):
+    if not fast_shapes(context, queries, w_out):
+        return plain_body(context, w_kv, queries, gain, w_out)
+    return fast_body(context, w_kv, queries, gain, w_out)
+
+
+def fast_body(context, w_kv, queries, gain, w_out):
+    _, size, _ = queries.shape
+    rows = context.shape[0]
+    head_count = lax.axis_size("head")
+    ctx_count = lax.axis_size("ctx")
+    pieces = ctx_count * lax.axis_size("groups")
+    chunk_heads = CHUNKS
+    starts = [sum(chunk_heads[:n]) for n in range(len(chunk_heads))]
+
+    received = []
+    for n, heads in enumerate(chunk_heads):
+        parts = project(context, w_kv, w_out if n == 0 else None, starts[n], heads, size, pieces)
+        moved = [partner(parts[s], "head", s) for s in range(head_count - 1, 0, -1)][::-1]
+        received.append([parts[0]] + moved)
+    w_full = gather_w_out(received[0], rows, w_out, pieces)
+
+    finished = []
+    for n in range(len(chunk_heads)):
+        state = None
+        for s in range(head_count):
+            state = attend(queries, [received[n][s]], state, rows, starts[n], s == head_count - 1)
+        level = 0
+        while (ctx_count >> level) > 1:
+            got = partner(state[0], "ctx", 1 << level)
+            level += 1
+            state = merge(level, got, *state[1:])
+        finished.append(
+            [partner(state[s], "head", s) if s else state[s] for s in range(head_count)]
+        )
+    return output(finished, chunk_heads, gain, w_full)
+
+
+CHUNKS = [2, 2]
+
+
 def solution(mesh):
     return jax.shard_map(
         body,

time: 185 us -> 83.7 us (0.45)
  waiting for transfers between devices: 67.4 us -> 31.5 us
  local copies, waits for them, and re-layouts: 32 us -> 4.29 us
  blocking collectives: 23.5 us -> 0 us
  matrix products: 22.1 us -> 0 us
  Pallas kernels: 0 us -> 21.5 us
  starting transfers between devices: 6.43 us -> 26 us
  between operations: 15 us -> 0.18 us
  other arithmetic: 11.3 us -> 0 us
  loops' own time: 6.81 us -> 0 us
    ppermute x0 -> x20, waiting for transfers between devices: none -> 31.5 us  [partner(): return lax.ppermute(value, axis, [(i, i ^ step) for i in range(count)])]
    ppermute x0 -> x20, starting transfers between devices: none -> 26 us  [partner(): return lax.ppermute(value, axis, [(i, i ^ step) for i in range(count)])]
    reduce_scatter x1 -> x0, waiting for transfers between devices: 25.6 us -> none  [body(): lax.psum_scatter(scaled.astype(jnp.bfloat16), 'ctx', scatter_dimension=1,...]
    all_to_all x1 -> x0, waiting for transfers between devices: 24.4 us -> none  [body(): lax.all_to_all(projected, 'head', split_axis=1, concat_axis=0, tiled=True)]
    dot_general x10 -> x0, matrix products: 22.1 us -> none  [the longest x4 10.3 us: attend(): jnp.einsum('hqk,khd->hqd', weights.astype(jnp.bfloat16), value_rows, pref...]
    pallas_call x0 -> x18, Pallas kernels: none -> 21.5 us  [call(): pl.pallas_call(kernel, out_shape=out_shape, in_specs=in_specs or [vmem] *...]
    unnamed x4 -> x0, waiting for transfers between devices: 17.4 us -> none
    all_to_all x1 -> x0, blocking collectives: 13.1 us -> none  [body(): lax.all_to_all(packed.astype(jnp.bfloat16), 'head', split_axis=1, concat_...]
  transfers between devices with their start and end apart: 4 -> 20, of which waited for: 3 -> 7; matrix products, arithmetic and copies ran while one was open for 5% -> 0% of each run, Pallas kernels for 0% -> 21%
where the time goes in v1:
time: 83.7 us; the launch traced here: 83.5 us
  waiting for transfers between devices  31.5 us (38%)
  starting transfers between devices  26 us (31%)
  Pallas kernels  21.5 us (26%)
  local copies, waits for them, and re-layouts  4.29 us (5%)
    ppermute x20, waiting for transfers between devices, partner(): return lax.ppermute(value, axis, [(i, i ^ step) for i in range(count)])  31.5 us
    ppermute x20, starting transfers between devices, partner(): return lax.ppermute(value, axis, [(i, i ^ step) for i in range(count)])  26 us
    pallas_call x18, Pallas kernels, call(): pl.pallas_call(kernel, out_shape=out_shape, in_specs=in_specs or [vmem] *...  21.5 us
    unnamed x14, local copies, waits for them, and re-layouts  4.29 us
  transfers between devices with their start and end apart: 20, of which 7 were waited for; matrix products, arithmetic and copies ran while one was open for 0% of the time, Pallas kernels for 21%

profile of v1, /device:TPU:0, one launch (start us, length us, event | category | flops | bytes accessed | tf_op | source)
XLA Modules:
  0.0 83.5 jit_solution(2123580988000853816)
XLA Ops:
  0.0 2.2 %copy-done.1 = bf16[1024,2048]{1,0:T(8,128)(2,1)S(1)} copy-done((bf16[1024,2048]{1,0:T(8,128)(2,1)S(1)}, bf16[1024,2048]{1,0:T(8,128)(2,1)}, u32[]{:S(2)}) %copy-start.1) | copy-done | bytes 4194328
  2.2 1.0 %copy-done.3 = bf16[256,1024]{1,0:T(8,128)(2,1)S(1)} copy-done((bf16[256,1024]{1,0:T(8,128)(2,1)S(1)}, bf16[256,1024]{1,0:T(8,128)(2,1)}, u32[]{:S(2)}) %copy-start.3) | copy-done | bytes 524312
  3.2 1.0 %copy-done.5 = bf16[256,1024]{1,0:T(8,128)(2,1)S(1)} copy-done((bf16[256,1024]{1,0:T(8,128)(2,1)S(1)}, bf16[256,1024]{1,0:T(8,128)(2,1)}, u32[]{:S(2)}) %copy-start.5) | copy-done | bytes 524312
  4.3 2.0 %shard_map.55 = (bf16[384,256]{1,0:T(8,128)(2,1)S(1)}, bf16[384,256]{1,0:T(8,128)(2,1)S(1)}, bf16[384,256]{1,0:T(8,128)(2,1)S(1)}, bf16[384,256]{1,0:T(8,128)(2,1)S(1)}) custom-call(bf16[256,1024]{1,0:T(8,128)(2,1)S(1)} %copy-done.3, bf16[1024,2048]{1,0:T(8,128)(2,1)S(1)} %copy-done.1, bf16[256,1024]{1,0:T(8,128)(2,1)S(1)} %copy-done.5), custom_call_target="tpu_custom_call" | custom-call | flops 536870912 | bytes 5242880 | tf_op jit(solution)/shard_map/pallas_call | solution.py:23
  6.3 0.0 copy-start
  6.3 5.1 %collective-permute-start = (bf16[384,256]{1,0:T(8,128)(2,1)S(1)}, bf16[384,256]{1,0:T(8,128)(2,1)S(1)}, u32[]{:S(2)}, u32[]{:S(2)}) collective-permute-start(bf16[384,256]{1,0:T(8,128)(2,1)S(1)} %get-tuple-element.45), channel_id=1, source_target_pairs={{0,3},{1,2},{2,1},{3,0},{4,7},{5,6},{6,5},{7,4},{8,11},{9,10},{10,... | collective-permute-start | bytes 589832 | tf_op jit(solution)/shard_map/ppermute | solution.py:42
  11.5 0.0 collective-permute-start.1
  11.5 0.6 collective-permute-start.2
  12.1 5.3 %collective-permute-done.rest_0_.refs_3_ = bf16[384,256]{1,0:T(8,128)(2,1)S(1)} collective-permute-done((bf16[384,256]{1,0:T(8,128)(2,1)S(1)}, bf16[384,256]{1,0:T(8,128)(2,1)S(1)}, u32[]{:S(2)}, u32[]{:S(2)}) %collective-permute-start) | collective-permute-done | bytes 196640 | tf_op jit(solution)/shard_map/ppermute | solution.py:42
  17.4 10.8 %collective-permute-done.1.rest_0_.refs_2_ = bf16[384,256]{1,0:T(8,128)(2,1)S(1)} collective-permute-done((bf16[384,256]{1,0:T(8,128)(2,1)S(1)}, bf16[384,256]{1,0:T(8,128)(2,1)S(1)}, u32[]{:S(2)}, u32[]{:S(2)}) %collective-permute-start.1) | collective-permute-done | bytes 196640 | tf_op jit(solution)/shard_map/ppermute | solution.py:42
  28.2 0.0 collective-permute-done.2.rest_0_.refs_1_
  28.2 1.6 %collective-permute-start.16 = (bf16[1,4,32,1024]{3,2,1,0:T(8,128)(2,1)S(1)}, bf16[1,4,32,1024]{3,2,1,0:T(8,128)(2,1)S(1)}, u32[]{:S(2)}, u32[]{:S(2)}) collective-permute-start(bf16[1,4,32,1024]{3,2,1,0:T(8,128)(2,1)S(1)} %bitcast.2), channel_id=1, source_target_pairs={{0,8},{4,12},{8,0},{12,4},{1,9},{5,13},{9,1},{13,5},{2,10},{6,14},... | collective-permute-start | bytes 786440 | tf_op jit(solution)/shard_map/ppermute | solution.py:42
  29.7 5.9 %collective-permute-done.16.b_ref = bf16[1,4,32,1024]{3,2,1,0:T(8,128)(2,1)S(1)} collective-permute-done((bf16[1,4,32,1024]{3,2,1,0:T(8,128)(2,1)S(1)}, bf16[1,4,32,1024]{3,2,1,0:T(8,128)(2,1)S(1)}, u32[]{:S(2)}, u32[]{:S(2)}) %collective-permute-start.16) | collective-permute-done | bytes 262176 | tf_op jit(solution)/shard_map/ppermute | solution.py:42
  35.7 1.6 %collective-permute-start.17 = (bf16[2,4,32,1024]{3,2,1,0:T(8,128)(2,1)S(1)}, bf16[2,4,32,1024]{3,2,1,0:T(8,128)(2,1)S(1)}, u32[]{:S(2)}, u32[]{:S(2)}) collective-permute-start(bf16[2,4,32,1024]{3,2,1,0:T(8,128)(2,1)S(1)} %shard_map.70.refs_0_), channel_id=1, source_target_pairs={{0,16},{16,0},{1,17},{17,1},{2,18},{18,2},{3,19},{19,3},{4,20},{20... | collective-permute-start | bytes 1572872 | tf_op jit(solution)/shard_map/ppermute | solution.py:42
  37.2 0.0 copy-done.2
  37.3 0.0 copy-done.4
  37.3 2.0 %shard_map.62 = (bf16[256,256]{1,0:T(8,128)(2,1)S(1)}, bf16[256,256]{1,0:T(8,128)(2,1)S(1)}, bf16[256,256]{1,0:T(8,128)(2,1)S(1)}, bf16[256,256]{1,0:T(8,128)(2,1)S(1)}) custom-call(bf16[256,1024]{1,0:T(8,128)(2,1)S(1)} %copy-done.4, bf16[1024,2048]{1,0:T(8,128)(2,1)S(1)} %copy-done.2), custom_call_target="tpu_custom_call" | custom-call | flops 536870912 | bytes 4718592 | tf_op jit(solution)/shard_map/pallas_call | solution.py:23
  39.3 0.1 collective-permute-start.10
  39.4 2.8 %collective-permute-start.9 = (bf16[256,256]{1,0:T(8,128)(2,1)S(1)}, bf16[256,256]{1,0:T(8,128)(2,1)S(1)}, u32[]{:S(2)}, u32[]{:S(2)}) collective-permute-start(bf16[256,256]{1,0:T(8,128)(2,1)S(1)} %get-tuple-element.66), channel_id=1, source_target_pairs={{0,2},{1,3},{2,0},{3,1},{4,6},{5,7},{6,4},{7,5},{8,10},{9,11},{10,... | collective-permute-start | bytes 393224 | tf_op jit(solution)/shard_map/ppermute | solution.py:42
  42.2 1.5 %collective-permute-start.8 = (bf16[256,256]{1,0:T(8,128)(2,1)S(1)}, bf16[256,256]{1,0:T(8,128)(2,1)S(1)}, u32[]{:S(2)}, u32[]{:S(2)}) collective-permute-start(bf16[256,256]{1,0:T(8,128)(2,1)S(1)} %get-tuple-element.65), channel_id=1, source_target_pairs={{0,3},{1,2},{2,1},{3,0},{4,7},{5,6},{6,5},{7,4},{8,11},{9,10},{10,... | collective-permute-start | bytes 393224 | tf_op jit(solution)/shard_map/ppermute | solution.py:42
  43.7 0.0 copy-done
  43.7 1.7 %shard_map.56 = (f32[2,64,2048]{2,1,0:T(8,128)S(1)}, f32[2,2,2048]{2,1,0:T(2,128)S(1)}) custom-call(bf16[4,64,2048]{2,1,0:T(8,128)(2,1)S(1)} %copy-done, bf16[384,256]{1,0:T(8,128)(2,1)S(1)} %get-tuple-element.48.rest_0_.refs_0_), custom_call_target="tpu_custom_call" | custom-call | flops 268435456 | bytes 1245184 | tf_op jit(solution)/shard_map/pallas_call | solution.py:23
  45.5 1.8 %shard_map.63 = (f32[2,64,2048]{2,1,0:T(8,128)S(1)}, f32[2,2,2048]{2,1,0:T(2,128)S(1)}) custom-call(bf16[4,64,2048]{2,1,0:T(8,128)(2,1)S(1)} %copy-done, bf16[256,256]{1,0:T(8,128)(2,1)S(1)} %get-tuple-element.68.rest_0_), custom_call_target="tpu_custom_call" | custom-call | flops 268435456 | bytes 1179648 | tf_op jit(solution)/shard_map/pallas_call | solution.py:23
  47.2 0.0 collective-permute-done.10.rest_0_
  47.3 1.9 %shard_map.64 = (f32[2,64,2048]{2,1,0:T(8,128)S(1)}, f32[2,2,2048]{2,1,0:T(2,128)S(1)}) custom-call(bf16[4,64,2048]{2,1,0:T(8,128)(2,1)S(1)} %copy-done, bf16[256,256]{1,0:T(8,128)(2,1)S(1)} %collective-permute-done.10.rest_0_, f32[2,64,2048]{2,1,0:T(8,128)S(1)} %get-tuple-element.69.rest_1_, f32[2,2,2048]{2,1,0:T(2,128)S(1)} %get-tuple-element.70.rest_2_), custom_call_target="tpu_custom_call" | custom-call | flops 268435456 | bytes 2260992 | tf_op jit(solution)/shard_map/pallas_call | solution.py:23
  49.1 1.7 %collective-permute-done.9.rest_0_ = bf16[256,256]{1,0:T(8,128)(2,1)S(1)} collective-permute-done((bf16[256,256]{1,0:T(8,128)(2,1)S(1)}, bf16[256,256]{1,0:T(8,128)(2,1)S(1)}, u32[]{:S(2)}, u32[]{:S(2)}) %collective-permute-start.9) | collective-permute-done | bytes 131104 | tf_op jit(solution)/shard_map/ppermute | solution.py:42
  50.8 1.9 %shard_map.65 = (f32[2,64,2048]{2,1,0:T(8,128)S(1)}, f32[2,2,2048]{2,1,0:T(2,128)S(1)}) custom-call(bf16[4,64,2048]{2,1,0:T(8,128)(2,1)S(1)} %copy-done, bf16[256,256]{1,0:T(8,128)(2,1)S(1)} %collective-permute-done.9.rest_0_, f32[2,64,2048]{2,1,0:T(8,128)S(1)} %get-tuple-element.71.rest_1_, f32[2,2,2048]{2,1,0:T(2,128)S(1)} %get-tuple-element.72.rest_2_), custom_call_target="tpu_custom_call" | custom-call | flops 268435456 | bytes 2260992 | tf_op jit(solution)/shard_map/pallas_call | solution.py:23
  52.7 0.1 collective-permute-start.18
  52.8 0.0 collective-permute-done.17.refs_1_
  52.8 0.5 collective-permute-start.19
  53.3 0.0 collective-permute-done.8.rest_0_
  53.3 2.0 %shard_map.66 = (bf16[2,72,1024]{2,1,0:T(8,128)(2,1)S(1)}, f32[2,64,1024]{2,1,0:T(8,128)S(1)}, f32[2,2,1024]{2,1,0:T(2,128)S(1)}) custom-call(bf16[4,64,2048]{2,1,0:T(8,128)(2,1)S(1)} %copy-done, bf16[256,256]{1,0:T(8,128)(2,1)S(1)} %collective-permute-done.8.rest_0_, f32[2,64,2048]{2,1,0:T(8,128)S(1)} %get-tuple-element.73.rest_1_, ...), custom_call_target="tpu_custom_call" | custom-call | flops 268435456 | bytes 2260992 | tf_op jit(solution)/shard_map/pallas_call | solution.py:23
  55.3 0.2 collective-permute-start.11
  55.4 1.9 %shard_map.57 = (f32[2,64,2048]{2,1,0:T(8,128)S(1)}, f32[2,2,2048]{2,1,0:T(2,128)S(1)}) custom-call(bf16[4,64,2048]{2,1,0:T(8,128)(2,1)S(1)} %copy-done, bf16[384,256]{1,0:T(8,128)(2,1)S(1)} %collective-permute-done.2.rest_0_.refs_1_, f32[2,64,2048]{2,1,0:T(8,128)S(1)} %get-tuple-element.49.rest_1_, f32[2,2,2048]{2,1,0:T(2,128)S(1)} %get-tuple-element.50.rest_2_), custom_call_target="tpu_custom_call" | custom-call | flops 268435456 | bytes 2326528 | tf_op jit(solution)/shard_map/pallas_call | solution.py:23
  57.3 1.9 %shard_map.58 = (f32[2,64,2048]{2,1,0:T(8,128)S(1)}, f32[2,2,2048]{2,1,0:T(2,128)S(1)}) custom-call(bf16[4,64,2048]{2,1,0:T(8,128)(2,1)S(1)} %copy-done, bf16[384,256]{1,0:T(8,128)(2,1)S(1)} %collective-permute-done.1.rest_0_.refs_2_, f32[2,64,2048]{2,1,0:T(8,128)S(1)} %get-tuple-element.51.rest_1_, f32[2,2,2048]{2,1,0:T(2,128)S(1)} %get-tuple-element.52.rest_2_), custom_call_target="tpu_custom_call" | custom-call | flops 268435456 | bytes 2326528 | tf_op jit(solution)/shard_map/pallas_call | solution.py:23
  59.2 2.1 %shard_map.59 = (bf16[2,72,1024]{2,1,0:T(8,128)(2,1)S(1)}, f32[2,64,1024]{2,1,0:T(8,128)S(1)}, f32[2,2,1024]{2,1,0:T(2,128)S(1)}) custom-call(bf16[4,64,2048]{2,1,0:T(8,128)(2,1)S(1)} %copy-done, bf16[384,256]{1,0:T(8,128)(2,1)S(1)} %collective-permute-done.rest_0_.refs_3_, f32[2,64,2048]{2,1,0:T(8,128)S(1)} %get-tuple-element.53.rest_1_, ...), custom_call_target="tpu_custom_call" | custom-call | flops 268435456 | bytes 2326528 | tf_op jit(solution)/shard_map/pallas_call | solution.py:23
  61.3 0.5 collective-permute-start.3
  61.8 0.0 collective-permute-done.11.got_ref
  61.8 0.2 shard_map.67
  62.0 1.6 %collective-permute-start.12 = (bf16[2,72,512]{2,1,0:T(8,128)(2,1)S(1)}, bf16[2,72,512]{2,1,0:T(8,128)(2,1)S(1)}, u32[]{:S(2)}, u32[]{:S(2)}) collective-permute-start(bf16[2,72,512]{2,1,0:T(8,128)(2,1)S(1)} %get-tuple-element.78), channel_id=1, source_target_pairs={{0,8},{4,12},{8,0},{12,4},{1,9},{5,13},{9,1},{13,5},{2,10},{6,14},... | collective-permute-start | bytes 442376 | tf_op jit(solution)/shard_map/ppermute | solution.py:42
  63.5 0.0 collective-permute-done.3.got_ref
  63.5 0.2 shard_map.60
  63.7 1.0 %collective-permute-start.4 = (bf16[2,72,512]{2,1,0:T(8,128)(2,1)S(1)}, bf16[2,72,512]{2,1,0:T(8,128)(2,1)S(1)}, u32[]{:S(2)}, u32[]{:S(2)}) collective-permute-start(bf16[2,72,512]{2,1,0:T(8,128)(2,1)S(1)} %get-tuple-element.58), channel_id=1, source_target_pairs={{0,8},{4,12},{8,0},{12,4},{1,9},{5,13},{9,1},{13,5},{2,10},{6,14},... | collective-permute-start | bytes 442376 | tf_op jit(solution)/shard_map/ppermute | solution.py:42
  64.7 4.0 %collective-permute-done.12.got_ref = bf16[2,72,512]{2,1,0:T(8,128)(2,1)S(1)} collective-permute-done((bf16[2,72,512]{2,1,0:T(8,128)(2,1)S(1)}, bf16[2,72,512]{2,1,0:T(8,128)(2,1)S(1)}, u32[]{:S(2)}, u32[]{:S(2)}) %collective-permute-start.12) | collective-permute-done | bytes 147488 | tf_op jit(solution)/shard_map/ppermute | solution.py:42
  68.8 0.1 shard_map.68
  68.8 0.1 collective-permute-start.13
  68.9 2.7 %collective-permute-start.14 = (bf16[2,64,128]{2,1,0:T(8,128)(2,1)S(1)}, bf16[2,64,128]{2,1,0:T(8,128)(2,1)S(1)}, u32[]{:S(2)}, u32[]{:S(2)}) collective-permute-start(bf16[2,64,128]{2,1,0:T(8,128)(2,1)S(1)} %get-tuple-element.83), channel_id=1, source_target_pairs={{0,2},{1,3},{2,0},{3,1},{4,6},{5,7},{6,4},{7,5},{8,10},{9,11},{10,... | collective-permute-start | bytes 98312 | tf_op jit(solution)/shard_map/ppermute | solution.py:42
  71.6 0.0 collective-permute-done.4.got_ref
  71.6 1.7 %collective-permute-start.15 = (bf16[2,64,128]{2,1,0:T(8,128)(2,1)S(1)}, bf16[2,64,128]{2,1,0:T(8,128)(2,1)S(1)}, u32[]{:S(2)}, u32[]{:S(2)}) collective-permute-start(bf16[2,64,128]{2,1,0:T(8,128)(2,1)S(1)} %get-tuple-element.84), channel_id=1, source_target_pairs={{0,3},{1,2},{2,1},{3,0},{4,7},{5,6},{6,5},{7,4},{8,11},{9,10},{10,... | collective-permute-start | bytes 98312 | tf_op jit(solution)/shard_map/ppermute | solution.py:42
  73.3 0.1 shard_map.61
  73.4 0.0 collective-permute-done.13.refs_5_
  73.4 0.1 collective-permute-start.5
  73.5 0.0 collective-permute-done.18.refs_2_
  73.5 2.7 %collective-permute-start.6 = (bf16[2,64,128]{2,1,0:T(8,128)(2,1)S(1)}, bf16[2,64,128]{2,1,0:T(8,128)(2,1)S(1)}, u32[]{:S(2)}, u32[]{:S(2)}) collective-permute-start(bf16[2,64,128]{2,1,0:T(8,128)(2,1)S(1)} %get-tuple-element.63), channel_id=1, source_target_pairs={{0,2},{1,3},{2,0},{3,1},{4,6},{5,7},{6,4},{7,5},{8,10},{9,11},{10,... | collective-permute-start | bytes 98312 | tf_op jit(solution)/shard_map/ppermute | solution.py:42
  76.1 0.0 collective-permute-done.19.refs_3_
  76.1 1.7 %collective-permute-start.7 = (bf16[2,64,128]{2,1,0:T(8,128)(2,1)S(1)}, bf16[2,64,128]{2,1,0:T(8,128)(2,1)S(1)}, u32[]{:S(2)}, u32[]{:S(2)}) collective-permute-start(bf16[2,64,128]{2,1,0:T(8,128)(2,1)S(1)} %get-tuple-element.64), channel_id=1, source_target_pairs={{0,3},{1,2},{2,1},{3,0},{4,7},{5,6},{6,5},{7,4},{8,11},{9,10},{10,... | collective-permute-start | bytes 98312 | tf_op jit(solution)/shard_map/ppermute | solution.py:42
  77.9 0.2 shard_map.71.refs_9_
  78.0 0.0 collective-permute-done.14.refs_6_
  78.0 0.0 collective-permute-done.15.refs_7_
  78.0 0.0 collective-permute-done.5.refs_1_
  78.0 0.3 collective-permute-done.6.refs_2_
  78.4 3.5 %collective-permute-done.7.refs_3_ = bf16[2,64,128]{2,1,0:T(8,128)(2,1)S(1)} collective-permute-done((bf16[2,64,128]{2,1,0:T(8,128)(2,1)S(1)}, bf16[2,64,128]{2,1,0:T(8,128)(2,1)S(1)}, u32[]{:S(2)}, u32[]{:S(2)}) %collective-permute-start.7) | collective-permute-done | bytes 32800 | tf_op jit(solution)/shard_map/ppermute | solution.py:42
  81.9 0.0 copy-done.6
  81.9 1.6 %shard_map.72 = bf16[128,1024]{1,0:T(8,128)(2,1)} custom-call(bf16[2,64,128]{2,1,0:T(8,128)(2,1)S(1)} %get-tuple-element.61.refs_0_, bf16[2,64,128]{2,1,0:T(8,128)(2,1)S(1)} %collective-permute-done.5.refs_1_, bf16[2,64,128]{2,1,0:T(8,128)(2,1)S(1)} %collective-permute-done.6.refs_2_, bf16[2,64,128]{2,1,0:T(8,128)(2,1)S(1)} %collective-permute-done.7.refs_3_, ...), custom_call_target="tpu_custom_call" | custom-call | flops 268435456 | bytes 2363392 | tf_op jit(solution)/shard_map/pallas_call | solution.py:23
  (8 shorter events, 0.1 us)
Async XLA Ops:
  0.0 2.2 %copy-start.1 = (bf16[1024,2048]{1,0:T(8,128)(2,1)S(1)}, bf16[1024,2048]{1,0:T(8,128)(2,1)}, u32[]{:S(2)}) copy-start(bf16[1024,2048]{1,0:T(8,128)(2,1)} %w_ref.3) | copy-start | bytes 12582916
  2.2 1.0 %copy-start.3 = (bf16[256,1024]{1,0:T(8,128)(2,1)S(1)}, bf16[256,1024]{1,0:T(8,128)(2,1)}, u32[]{:S(2)}) copy-start(bf16[256,1024]{1,0:T(8,128)(2,1)} %x_ref.3) | copy-start | bytes 1572868
  3.2 1.0 %copy-start.5 = (bf16[256,1024]{1,0:T(8,128)(2,1)S(1)}, bf16[256,1024]{1,0:T(8,128)(2,1)}, u32[]{:S(2)}) copy-start(bf16[256,1024]{1,0:T(8,128)(2,1)} %rest_0_.1) | copy-start | bytes 1572868
  4.3 33.0 %copy-start.2 = (bf16[1024,2048]{1,0:T(8,128)(2,1)S(1)}, bf16[1024,2048]{1,0:T(8,128)(2,1)}, u32[]{:S(2)}) copy-start(bf16[1024,2048]{1,0:T(8,128)(2,1)} %w_ref.3) | copy-start | bytes 12582916
  4.3 33.0 %copy-start.4 = (bf16[256,1024]{1,0:T(8,128)(2,1)S(1)}, bf16[256,1024]{1,0:T(8,128)(2,1)}, u32[]{:S(2)}) copy-start(bf16[256,1024]{1,0:T(8,128)(2,1)} %x_ref.3) | copy-start | bytes 1572868
  6.3 37.4 %copy-start = (bf16[4,64,2048]{2,1,0:T(8,128)(2,1)S(1)}, bf16[4,64,2048]{2,1,0:T(8,128)(2,1)}, u32[]{:S(2)}) copy-start(bf16[4,64,2048]{2,1,0:T(8,128)(2,1)} %q_ref.15) | copy-start | bytes 3145732
  6.3 11.0 %collective-permute-start = (bf16[384,256]{1,0:T(8,128)(2,1)S(1)}, bf16[384,256]{1,0:T(8,128)(2,1)S(1)}, u32[]{:S(2)}, u32[]{:S(2)}) collective-permute-start(bf16[384,256]{1,0:T(8,128)(2,1)S(1)} %get-tuple-element.45), channel_id=1, source_target_pairs={{0,3},{1,2},{2,1},{3,0},{4,7},{5,6},{6,5},{7,4},{8,11},{9,10},{10,... | collective-permute-start | bytes 589832 | tf_op jit(solution)/shard_map/ppermute | solution.py:42
  11.5 16.7 %collective-permute-start.1 = (bf16[384,256]{1,0:T(8,128)(2,1)S(1)}, bf16[384,256]{1,0:T(8,128)(2,1)S(1)}, u32[]{:S(2)}, u32[]{:S(2)}) collective-permute-start(bf16[384,256]{1,0:T(8,128)(2,1)S(1)} %get-tuple-element.46), channel_id=1, source_target_pairs={{0,2},{1,3},{2,0},{3,1},{4,6},{5,7},{6,4},{7,5},{8,10},{9,11},{10,... | collective-permute-start | bytes 589832 | tf_op jit(solution)/shard_map/ppermute | solution.py:42
  11.5 16.7 %collective-permute-start.2 = (bf16[384,256]{1,0:T(8,128)(2,1)S(1)}, bf16[384,256]{1,0:T(8,128)(2,1)S(1)}, u32[]{:S(2)}, u32[]{:S(2)}) collective-permute-start(bf16[384,256]{1,0:T(8,128)(2,1)S(1)} %get-tuple-element.47), channel_id=1, source_target_pairs={{0,1},{1,0},{2,3},{3,2},{4,5},{5,4},{6,7},{7,6},{8,9},{9,8},{10,11... | collective-permute-start | bytes 589832 | tf_op jit(solution)/shard_map/ppermute | solution.py:42
  28.2 7.4 %collective-permute-start.16 = (bf16[1,4,32,1024]{3,2,1,0:T(8,128)(2,1)S(1)}, bf16[1,4,32,1024]{3,2,1,0:T(8,128)(2,1)S(1)}, u32[]{:S(2)}, u32[]{:S(2)}) collective-permute-start(bf16[1,4,32,1024]{3,2,1,0:T(8,128)(2,1)S(1)} %bitcast.2), channel_id=1, source_target_pairs={{0,8},{4,12},{8,0},{12,4},{1,9},{5,13},{9,1},{13,5},{2,10},{6,14},... | collective-permute-start | bytes 786440 | tf_op jit(solution)/shard_map/ppermute | solution.py:42
  35.7 17.1 %collective-permute-start.17 = (bf16[2,4,32,1024]{3,2,1,0:T(8,128)(2,1)S(1)}, bf16[2,4,32,1024]{3,2,1,0:T(8,128)(2,1)S(1)}, u32[]{:S(2)}, u32[]{:S(2)}) collective-permute-start(bf16[2,4,32,1024]{3,2,1,0:T(8,128)(2,1)S(1)} %shard_map.70.refs_0_), channel_id=1, source_target_pairs={{0,16},{16,0},{1,17},{17,1},{2,18},{18,2},{3,19},{19,3},{4,20},{20... | collective-permute-start | bytes 1572872 | tf_op jit(solution)/shard_map/ppermute | solution.py:42
  39.3 8.0 %collective-permute-start.10 = (bf16[256,256]{1,0:T(8,128)(2,1)S(1)}, bf16[256,256]{1,0:T(8,128)(2,1)S(1)}, u32[]{:S(2)}, u32[]{:S(2)}) collective-permute-start(bf16[256,256]{1,0:T(8,128)(2,1)S(1)} %get-tuple-element.67), channel_id=1, source_target_pairs={{0,1},{1,0},{2,3},{3,2},{4,5},{5,4},{6,7},{7,6},{8,9},{9,8},{10,11... | collective-permute-start | bytes 393224 | tf_op jit(solution)/shard_map/ppermute | solution.py:42
  39.4 11.5 %collective-permute-start.9 = (bf16[256,256]{1,0:T(8,128)(2,1)S(1)}, bf16[256,256]{1,0:T(8,128)(2,1)S(1)}, u32[]{:S(2)}, u32[]{:S(2)}) collective-permute-start(bf16[256,256]{1,0:T(8,128)(2,1)S(1)} %get-tuple-element.66), channel_id=1, source_target_pairs={{0,2},{1,3},{2,0},{3,1},{4,6},{5,7},{6,4},{7,5},{8,10},{9,11},{10,... | collective-permute-start | bytes 393224 | tf_op jit(solution)/shard_map/ppermute | solution.py:42
  42.2 11.1 %collective-permute-start.8 = (bf16[256,256]{1,0:T(8,128)(2,1)S(1)}, bf16[256,256]{1,0:T(8,128)(2,1)S(1)}, u32[]{:S(2)}, u32[]{:S(2)}) collective-permute-start(bf16[256,256]{1,0:T(8,128)(2,1)S(1)} %get-tuple-element.65), channel_id=1, source_target_pairs={{0,3},{1,2},{2,1},{3,0},{4,7},{5,6},{6,5},{7,4},{8,11},{9,10},{10,... | collective-permute-start | bytes 393224 | tf_op jit(solution)/shard_map/ppermute | solution.py:42
  52.7 20.8 %collective-permute-start.18 = (bf16[2,4,32,1024]{3,2,1,0:T(8,128)(2,1)S(1)}, bf16[2,4,32,1024]{3,2,1,0:T(8,128)(2,1)S(1)}, u32[]{:S(2)}, u32[]{:S(2)}) collective-permute-start(bf16[2,4,32,1024]{3,2,1,0:T(8,128)(2,1)S(1)} %shard_map.70.refs_0_), channel_id=1, source_target_pairs={{0,4},{4,0},{8,12},{12,8},{1,5},{5,1},{9,13},{13,9},{2,6},{6,2},{1... | collective-permute-start | bytes 1572872 | tf_op jit(solution)/shard_map/ppermute | solution.py:42
  52.8 23.4 %collective-permute-start.19 = (bf16[2,4,32,1024]{3,2,1,0:T(8,128)(2,1)S(1)}, bf16[2,4,32,1024]{3,2,1,0:T(8,128)(2,1)S(1)}, u32[]{:S(2)}, u32[]{:S(2)}) collective-permute-start(bf16[2,4,32,1024]{3,2,1,0:T(8,128)(2,1)S(1)} %collective-permute-done.17.refs_1_), channel_id=1, source_target_pairs={{0,4},{4,0},{8,12},{12,8},{1,5},{5,1},{9,13},{13,9},{2,6},{6,2},{1... | collective-permute-start | bytes 1572872 | tf_op jit(solution)/shard_map/ppermute | solution.py:42
  55.3 6.5 %collective-permute-start.11 = (bf16[2,72,1024]{2,1,0:T(8,128)(2,1)S(1)}, bf16[2,72,1024]{2,1,0:T(8,128)(2,1)S(1)}, u32[]{:S(2)}, u32[]{:S(2)}) collective-permute-start(bf16[2,72,1024]{2,1,0:T(8,128)(2,1)S(1)} %get-tuple-element.75), channel_id=1, source_target_pairs={{0,4},{4,0},{8,12},{12,8},{1,5},{5,1},{9,13},{13,9},{2,6},{6,2},{1... | collective-permute-start | bytes 884744 | tf_op jit(solution)/shard_map/ppermute | solution.py:42
  59.2 22.7 %copy-start.6 = (f32[1024]{0:T(1024)S(1)}, f32[1024]{0:T(1024)}, u32[]{:S(2)}) copy-start(f32[1024]{0:T(1024)} %param.8) | copy-start | bytes 12292
  61.3 2.2 %collective-permute-start.3 = (bf16[2,72,1024]{2,1,0:T(8,128)(2,1)S(1)}, bf16[2,72,1024]{2,1,0:T(8,128)(2,1)S(1)}, u32[]{:S(2)}, u32[]{:S(2)}) collective-permute-start(bf16[2,72,1024]{2,1,0:T(8,128)(2,1)S(1)} %get-tuple-element.55), channel_id=1, source_target_pairs={{0,4},{4,0},{8,12},{12,8},{1,5},{5,1},{9,13},{13,9},{2,6},{6,2},{1... | collective-permute-start | bytes 884744 | tf_op jit(solution)/shard_map/ppermute | solution.py:42
  62.0 6.8 %collective-permute-start.12 = (bf16[2,72,512]{2,1,0:T(8,128)(2,1)S(1)}, bf16[2,72,512]{2,1,0:T(8,128)(2,1)S(1)}, u32[]{:S(2)}, u32[]{:S(2)}) collective-permute-start(bf16[2,72,512]{2,1,0:T(8,128)(2,1)S(1)} %get-tuple-element.78), channel_id=1, source_target_pairs={{0,8},{4,12},{8,0},{12,4},{1,9},{5,13},{9,1},{13,5},{2,10},{6,14},... | collective-permute-start | bytes 442376 | tf_op jit(solution)/shard_map/ppermute | solution.py:42
  63.7 7.9 %collective-permute-start.4 = (bf16[2,72,512]{2,1,0:T(8,128)(2,1)S(1)}, bf16[2,72,512]{2,1,0:T(8,128)(2,1)S(1)}, u32[]{:S(2)}, u32[]{:S(2)}) collective-permute-start(bf16[2,72,512]{2,1,0:T(8,128)(2,1)S(1)} %get-tuple-element.58), channel_id=1, source_target_pairs={{0,8},{4,12},{8,0},{12,4},{1,9},{5,13},{9,1},{13,5},{2,10},{6,14},... | collective-permute-start | bytes 442376 | tf_op jit(solution)/shard_map/ppermute | solution.py:42
  68.8 4.5 %collective-permute-start.13 = (bf16[2,64,128]{2,1,0:T(8,128)(2,1)S(1)}, bf16[2,64,128]{2,1,0:T(8,128)(2,1)S(1)}, u32[]{:S(2)}, u32[]{:S(2)}) collective-permute-start(bf16[2,64,128]{2,1,0:T(8,128)(2,1)S(1)} %get-tuple-element.82), channel_id=1, source_target_pairs={{0,1},{1,0},{2,3},{3,2},{4,5},{5,4},{6,7},{7,6},{8,9},{9,8},{10,11... | collective-permute-start | bytes 98312 | tf_op jit(solution)/shard_map/ppermute | solution.py:42
  68.9 9.1 %collective-permute-start.14 = (bf16[2,64,128]{2,1,0:T(8,128)(2,1)S(1)}, bf16[2,64,128]{2,1,0:T(8,128)(2,1)S(1)}, u32[]{:S(2)}, u32[]{:S(2)}) collective-permute-start(bf16[2,64,128]{2,1,0:T(8,128)(2,1)S(1)} %get-tuple-element.83), channel_id=1, source_target_pairs={{0,2},{1,3},{2,0},{3,1},{4,6},{5,7},{6,4},{7,5},{8,10},{9,11},{10,... | collective-permute-start | bytes 98312 | tf_op jit(solution)/shard_map/ppermute | solution.py:42
  71.6 6.4 %collective-permute-start.15 = (bf16[2,64,128]{2,1,0:T(8,128)(2,1)S(1)}, bf16[2,64,128]{2,1,0:T(8,128)(2,1)S(1)}, u32[]{:S(2)}, u32[]{:S(2)}) collective-permute-start(bf16[2,64,128]{2,1,0:T(8,128)(2,1)S(1)} %get-tuple-element.84), channel_id=1, source_target_pairs={{0,3},{1,2},{2,1},{3,0},{4,7},{5,6},{6,5},{7,4},{8,11},{9,10},{10,... | collective-permute-start | bytes 98312 | tf_op jit(solution)/shard_map/ppermute | solution.py:42
  73.4 4.6 %collective-permute-start.5 = (bf16[2,64,128]{2,1,0:T(8,128)(2,1)S(1)}, bf16[2,64,128]{2,1,0:T(8,128)(2,1)S(1)}, u32[]{:S(2)}, u32[]{:S(2)}) collective-permute-start(bf16[2,64,128]{2,1,0:T(8,128)(2,1)S(1)} %get-tuple-element.62), channel_id=1, source_target_pairs={{0,1},{1,0},{2,3},{3,2},{4,5},{5,4},{6,7},{7,6},{8,9},{9,8},{10,11... | collective-permute-start | bytes 98312 | tf_op jit(solution)/shard_map/ppermute | solution.py:42
  73.5 4.9 %collective-permute-start.6 = (bf16[2,64,128]{2,1,0:T(8,128)(2,1)S(1)}, bf16[2,64,128]{2,1,0:T(8,128)(2,1)S(1)}, u32[]{:S(2)}, u32[]{:S(2)}) collective-permute-start(bf16[2,64,128]{2,1,0:T(8,128)(2,1)S(1)} %get-tuple-element.63), channel_id=1, source_target_pairs={{0,2},{1,3},{2,0},{3,1},{4,6},{5,7},{6,4},{7,5},{8,10},{9,11},{10,... | collective-permute-start | bytes 98312 | tf_op jit(solution)/shard_map/ppermute | solution.py:42
  76.1 5.7 %collective-permute-start.7 = (bf16[2,64,128]{2,1,0:T(8,128)(2,1)S(1)}, bf16[2,64,128]{2,1,0:T(8,128)(2,1)S(1)}, u32[]{:S(2)}, u32[]{:S(2)}) collective-permute-start(bf16[2,64,128]{2,1,0:T(8,128)(2,1)S(1)} %get-tuple-element.64), channel_id=1, source_target_pairs={{0,3},{1,2},{2,1},{3,0},{4,7},{5,6},{6,5},{7,4},{8,11},{9,10},{10,... | collective-permute-start | bytes 98312 | tf_op jit(solution)/shard_map/ppermute | solution.py:42

commit v2 on v1

--- a/solution.py
+++ b/solution.py
@@ -42,12 +42,12 @@
     return lax.ppermute(value, axis, [(i, i ^ step) for i in range(count)])
 
 
-def project_kernel(total, offset, width, size, scale, piece, x_ref, w_ref, *rest):
+def project_kernel(total, offset, width, size, scale, x_hbm, w_ref, *rest):
     count = lax.axis_size("head")
-    carried_ref, rest = (rest[0], rest[1:]) if piece else (None, rest)
-    outs, slots, sems = rest[:count], rest[count], rest[count + 1]
-    rows = x_ref.shape[0]
+    outs, (x_ref, slots, x_sem, sems) = rest[:count], rest[count:]
     here = lax.axis_index("head")
+    fetch = pltpu.make_async_copy(x_hbm, x_ref, x_sem)
+    fetch.start()
     copies = []
     order = list(range(count - 1, -1, -1))
     for step in order:
@@ -58,36 +58,35 @@
         copies.append(copy)
     column = lax.broadcasted_iota(jnp.int32, (1, width), 1)
     factor = jnp.where(lax.rem(column, 2 * size) < size, scale, 1.0).astype(f32)
-    if piece:
-        place = lax.axis_index("groups") * lax.axis_size("ctx") + lax.axis_index("ctx")
-        own = carried_ref[pl.ds(pl.multiple_of(place * piece, piece), piece), :]
+    fetch.wait()
     for copy, step in zip(copies, order):
         copy.wait()
         product = jnp.dot(x_ref[...], slots[step], preferred_element_type=f32)
-        outs[step][0:rows, :] = (product * factor).astype(bf16)
-        if piece:
-            for j, at in enumerate(range(0, own.shape[1], width)):
-                part = own[:, at : at + width]
-                outs[step][rows + j * piece : rows + (j + 1) * piece, 0 : part.shape[1]] = part
-
-
-def project(context, w_kv, w_out, offset, heads, size, pieces):
+        outs[step][...] = (product * factor).astype(bf16)
+
+
+def project(context, w_kv, offset, heads, size):
     count = lax.axis_size("head")
     rows, depth = context.shape
     width = 2 * size * heads
     total = w_kv.shape[1] // count
-    piece = w_out.shape[0] // pieces if w_out is not None else 0
-    extra = piece * (-(-w_out.shape[1] // width)) if piece else 0
-    args = [context, w_kv] + ([w_out] if piece else [])
     return call(
         functools.partial(
-            project_kernel, total, 2 * size * offset, width, size, 1.0 / math.sqrt(size), piece
+            project_kernel, total, 2 * size * offset, width, size, 1.0 / math.sqrt(size)
         ),
-        [shape((rows + extra, width), bf16)] * count,
-        args,
+        [shape((rows, width), bf16)] * count,
+        [
+            pltpu.with_memory_space_constraint(context, pltpu.HBM),
+            pltpu.with_memory_space_constraint(w_kv, pltpu.HBM),
+        ],
         flops=2 * rows * depth * width * count,
-        scratch=[pltpu.VMEM((count, depth, width), bf16), pltpu.SemaphoreType.DMA((count,))],
-        in_specs=[vmem, in_hbm] + ([vmem] if piece else []),
+        scratch=[
+            pltpu.VMEM((rows, depth), bf16),
+            pltpu.VMEM((count, depth, width), bf16),
+            pltpu.SemaphoreType.DMA,
+            pltpu.SemaphoreType.DMA((count,)),
+        ],
+        in_specs=[in_hbm, in_hbm],
     )
 
 
@@ -269,109 +268,94 @@
     )
 
 
-def unpack_kernel(rows, piece, *refs):
-    out_ref = refs[-1]
-    columns = out_ref.shape[2]
-    for step, ref in enumerate(refs[:-1]):
-        width = ref.shape[1]
-        for j, at in enumerate(range(0, columns, width)):
-            wide = min(width, columns - at)
-            out_ref[step, :, at : at + wide] = ref[
-                rows + j * piece : rows + (j + 1) * piece, 0:wide
-            ]
-
-
-def pair_kernel(a_ref, b_ref, out_ref):
-    out_ref[0 : a_ref.shape[0]] = a_ref[...]
-    out_ref[a_ref.shape[0] :] = b_ref[...]
+def pick_kernel(piece, w_ref, out_ref, sem):
+    place = lax.axis_index("groups") * lax.axis_size("ctx") + lax.axis_index("ctx")
+    rows = pl.ds(pl.multiple_of(place * piece, piece), piece)
+    copy = pltpu.make_async_copy(w_ref.at[rows, :], out_ref, sem)
+    copy.start()
+    copy.wait()
+
+
+def stack_kernel(*refs):
+    for n, ref in enumerate(refs[:-1]):
+        refs[-1][n] = ref[...]
 
 
 def order_kernel(offsets, *refs):
     out_ref = refs[-1]
     place = lax.axis_index("groups") * lax.axis_size("ctx") + lax.axis_index("ctx")
-    j = 0
-    for ref in refs[:-1]:
-        piece = ref.shape[2]
-        for i in range(ref.shape[0]):
-            start = pl.multiple_of((place ^ offsets[j]) * piece, piece)
-            out_ref[:, pl.ds(start, piece), :] = ref[i]
-            j += 1
-
-
-def gather_w_out(parts, rows, w_out, pieces):
-    heads, columns = len(parts), w_out.shape[1]
-    piece = w_out.shape[0] // pieces
-    (held,) = call(
-        functools.partial(unpack_kernel, rows, piece), [shape((heads, piece, columns), bf16)], parts
-    )
-    held = held.reshape(1, heads, piece, columns)
+    for offset, ref in zip(offsets, refs[:-1]):
+        piece = ref.shape[1]
+        start = pl.multiple_of((place ^ offset) * piece, piece)
+        out_ref[:, pl.ds(start, piece), :] = ref[...]
+
+
+def gather_w_out(w_out, pieces):
+    heads, (rows, columns) = lax.axis_size("head"), w_out.shape
+    piece = rows // pieces
+    (own,) = call(
+        functools.partial(pick_kernel, piece),
+        [shape((piece, columns), bf16)],
+        [pltpu.with_memory_space_constraint(w_out, pltpu.HBM)],
+        scratch=[pltpu.SemaphoreType.DMA],
+        in_specs=[in_hbm],
+    )
+    moved = [partner(own, "head", s) for s in range(1, heads)]
+    held = list(call(stack_kernel, [shape((heads, piece, columns), bf16)], [own] + moved))
     ctx = lax.axis_size("ctx")
     steps = [("ctx", 1 << b, 1 << b) for b in range(1, (ctx - 1).bit_length())]
     steps += [
         ("groups", 1 << b, ctx << b) for b in range((lax.axis_size("groups") - 1).bit_length())
     ]
+    steps += [("ctx", 1, 1)]
     offsets = [0]
-    groups = [held]
-    for n, (axis, bit, weight) in enumerate(steps):
-        got = partner(held, axis, bit)
+    for axis, bit, weight in steps:
+        held = held + [partner(h, axis, bit) for h in held]
         offsets = offsets + [o ^ weight for o in offsets]
-        if n + 1 < len(steps):
-            (held,) = call(
-                pair_kernel, [shape((2 * held.shape[0],) + held.shape[1:], bf16)], [held, got]
-            )
-            groups = [held]
-        else:
-            groups = [held, got]
-    groups = groups + [partner(g, "ctx", 1) for g in groups]
-    offsets = offsets + [o ^ 1 for o in offsets]
     (full,) = call(
-        functools.partial(order_kernel, offsets),
-        [shape((heads, w_out.shape[0], columns), bf16)],
-        groups,
+        functools.partial(order_kernel, offsets), [shape((heads, rows, columns), bf16)], held
     )
     return full
 
 
-def output_kernel(chunk_heads, x_count, *refs):
-    out_ref = refs[-1]
-    gain_ref, w_ref = refs[x_count], refs[x_count + 1]
+def output_kernel(start, width, first, last, *refs):
     count = lax.axis_size("head")
     here = lax.axis_index("head")
-    size = refs[0].shape[1]
-    own = refs[0].shape[2]
-    width = w_ref.shape[0] * w_ref.shape[1]
-    blocks = []
-    square = jnp.zeros((1, own), f32)
+    blocks, (gain_ref, w_ref), rest = refs[:count], refs[count : count + 2], refs[count + 2 :]
+    heads, size, own = blocks[0].shape
+    rows = heads * size
+    square = jnp.zeros((1, own), f32) if first else rest[1][...]
+    result = jnp.zeros((own, w_ref.shape[2]), f32) if first else rest[0][...]
     for step in range(count):
-        start = 0
-        for n, heads in enumerate(chunk_heads):
-            block = refs[n * count + step][...].reshape(heads * size, own).astype(f32)
-            square += jnp.sum(block * block, axis=0, keepdims=True)
-            blocks.append((step, start * size, heads * size, block))
-            start += heads
+        block = blocks[step][...].reshape(rows, own).astype(f32)
+        square += jnp.sum(block * block, axis=0, keepdims=True)
+        gain = gain_ref[here ^ step, :, start : start + rows]
+        result += jnp.dot(
+            (block.T * gain).astype(bf16),
+            w_ref[step, start : start + rows, :],
+            preferred_element_type=f32,
+        )
+    if not last:
+        rest[-2][...] = result
+        rest[-1][...] = square
+        return
     factor = lax.rsqrt(square / width + epsilon)
     factor = jnp.broadcast_to(factor, (128, own)).T[:, 0:1]
-    result = jnp.zeros((own, w_ref.shape[2]), f32)
-    for step, start, rows, block in blocks:
-        gain = gain_ref[here ^ step, :, start : start + rows]
-        normed = (block.T * gain * factor).astype(bf16)
-        result += jnp.dot(
-            normed, w_ref[step, start : start + rows, :], preferred_element_type=f32
-        )
-    out_ref[...] = result.astype(bf16)
-
-
-def output(pieces, chunk_heads, gain, w_full):
+    rest[-1][...] = (result * factor).astype(bf16)
+
+
+def output(blocks, state, start, gain, w_full, last):
     count, rows, columns = w_full.shape
-    args = [p for chunk in pieces for p in chunk]
-    own = args[0].shape[2]
-    (result,) = call(
-        functools.partial(output_kernel, chunk_heads, len(args)),
-        [shape((own, columns), bf16)],
-        args + [gain.reshape(count, 1, rows), w_full],
-        flops=2 * own * count * rows * columns,
-    )
-    return result
+    heads, size, own = blocks[0].shape
+    out_shape = [shape((own, columns), bf16)] if last else [
+        shape((own, columns), f32), shape((1, own), f32)
+    ]
+    return call(
+        functools.partial(output_kernel, start * size, count * rows, state is None, last),
+        out_shape,
+        [*blocks, gain.reshape(count, 1, rows), w_full, *(state or ())],
+        flops=2 * own * count * heads * size * columns,
+    )
 
 
 def plain_body(context, w_kv, queries, gain, w_out):
@@ -482,10 +466,10 @@
 
     received = []
     for n, heads in enumerate(chunk_heads):
-        parts = project(context, w_kv, w_out if n == 0 else None, starts[n], heads, size, pieces)
+        parts = project(context, w_kv, starts[n], heads, size)
         moved = [partner(parts[s], "head", s) for s in range(head_count - 1, 0, -1)][::-1]
         received.append([parts[0]] + moved)
-    w_full = gather_w_out(received[0], rows, w_out, pieces)
+    w_full = gather_w_out(w_out, pieces)
 
     finished = []
     for n in range(len(chunk_heads)):
@@ -500,7 +484,11 @@
         finished.append(
             [partner(state[s], "head", s) if s else state[s] for s in range(head_count)]
         )
-    return output(finished, chunk_heads, gain, w_full)
+    state = None
+    for n in range(len(chunk_heads)):
+        last = n + 1 == len(chunk_heads)
+        state = output(finished[n], state, starts[n], gain, w_full, last)
+    return state[0]
 
 
 CHUNKS = [2, 2]

time: 83.7 us -> 80.7 us (0.964)
  waiting for transfers between devices: 31.5 us -> 24.3 us
  starting transfers between devices: 26 us -> 31.7 us
  local copies, waits for them, and re-layouts: 4.29 us -> 0.01 us
  Pallas kernels: 21.5 us -> 24.3 us
    ppermute x20 -> x26, waiting for transfers between devices: 31.5 us -> 24.3 us  [partner(): return lax.ppermute(value, axis, [(i, i ^ step) for i in range(count)])]
    ppermute x20 -> x26, starting transfers between devices: 26 us -> 31.7 us  [partner(): return lax.ppermute(value, axis, [(i, i ^ step) for i in range(count)])]
    unnamed x14 -> x4, local copies, waits for them, and re-layouts: 4.29 us -> 0.01 us
    pallas_call x18 -> x19, Pallas kernels: 21.5 us -> 24.3 us  [call(): pl.pallas_call(kernel, out_shape=out_shape, in_specs=in_specs or [vmem] *...]
  transfers between devices with their start and end apart: 20 -> 26, of which waited for: 7 -> 6; matrix products, arithmetic and copies ran while one was open for 0% -> 0% of each run, Pallas kernels for 21% -> 25%
where the time goes in v2:
time: 80.7 us; the launch traced here: 80.6 us
  starting transfers between devices  31.7 us (39%)
  Pallas kernels  24.3 us (30%)
  waiting for transfers between devices  24.3 us (30%)
    ppermute x26, starting transfers between devices, partner(): return lax.ppermute(value, axis, [(i, i ^ step) for i in range(count)])  31.7 us
    pallas_call x19, Pallas kernels, call(): pl.pallas_call(kernel, out_shape=out_shape, in_specs=in_specs or [vmem] *...  24.3 us
    ppermute x26, waiting for transfers between devices, partner(): return lax.ppermute(value, axis, [(i, i ^ step) for i in range(count)])  24.3 us
  transfers between devices with their start and end apart: 26, of which 6 were waited for; matrix products, arithmetic and copies ran while one was open for 0% of the time, Pallas kernels for 25%

profile of v2, /device:TPU:0, one launch (start us, length us, event | category | flops | bytes accessed | tf_op | source)
XLA Modules:
  0.0 80.6 jit_solution(13432672324134045211)
XLA Ops:
  0.0 3.0 %shard_map.65 = (bf16[256,256]{1,0:T(8,128)(2,1)S(1)}, bf16[256,256]{1,0:T(8,128)(2,1)S(1)}, bf16[256,256]{1,0:T(8,128)(2,1)S(1)}, bf16[256,256]{1,0:T(8,128)(2,1)S(1)}) custom-call(bf16[256,1024]{1,0:T(8,128)(2,1)} %x_hbm.3, bf16[1024,2048]{1,0:T(8,128)(2,1)} %w_ref.5), custom_call_target="tpu_custom_call" | custom-call | flops 536870912 | bytes 4718592 | tf_op jit(solution)/shard_map/pallas_call | solution.py:23
  3.0 4.1 %collective-permute-start.19 = (bf16[256,256]{1,0:T(8,128)(2,1)S(1)}, bf16[256,256]{1,0:T(8,128)(2,1)S(1)}, u32[]{:S(2)}, u32[]{:S(2)}) collective-permute-start(bf16[256,256]{1,0:T(8,128)(2,1)S(1)} %get-tuple-element.68), channel_id=1, source_target_pairs={{0,2},{1,3},{2,0},{3,1},{4,6},{5,7},{6,4},{7,5},{8,10},{9,11},{10,... | collective-permute-start | bytes 393224 | tf_op jit(solution)/shard_map/ppermute | solution.py:42
  7.2 0.8 %shard_map.62.refs_0_ = bf16[32,1024]{1,0:T(8,128)(2,1)S(1)} custom-call(bf16[256,1024]{1,0:T(8,128)(2,1)} %w_ref.4), custom_call_target="tpu_custom_call" | custom-call | bytes 524288 | tf_op jit(solution)/shard_map/pallas_call | solution.py:23
  8.0 1.6 %collective-permute-start.8 = (bf16[32,1024]{1,0:T(8,128)(2,1)S(1)}, bf16[32,1024]{1,0:T(8,128)(2,1)S(1)}, u32[]{:S(2)}, u32[]{:S(2)}) collective-permute-start(bf16[32,1024]{1,0:T(8,128)(2,1)S(1)} %shard_map.62.refs_0_), channel_id=1, source_target_pairs={{0,1},{1,0},{2,3},{3,2},{4,5},{5,4},{6,7},{7,6},{8,9},{9,8},{10,11... | collective-permute-start | bytes 196616 | tf_op jit(solution)/shard_map/ppermute | solution.py:42
  9.7 0.3 collective-permute-start.9
  10.0 2.5 %collective-permute-start.10 = (bf16[32,1024]{1,0:T(8,128)(2,1)S(1)}, bf16[32,1024]{1,0:T(8,128)(2,1)S(1)}, u32[]{:S(2)}, u32[]{:S(2)}) collective-permute-start(bf16[32,1024]{1,0:T(8,128)(2,1)S(1)} %shard_map.62.refs_0_), channel_id=1, source_target_pairs={{0,3},{1,2},{2,1},{3,0},{4,7},{5,6},{6,5},{7,4},{8,11},{9,10},{10,... | collective-permute-start | bytes 196616 | tf_op jit(solution)/shard_map/ppermute | solution.py:42
  12.5 0.7 collective-permute-start.20
  13.1 0.0 collective-permute-done.8.refs_1_
  13.1 0.9 %collective-permute-start.18 = (bf16[256,256]{1,0:T(8,128)(2,1)S(1)}, bf16[256,256]{1,0:T(8,128)(2,1)S(1)}, u32[]{:S(2)}, u32[]{:S(2)}) collective-permute-start(bf16[256,256]{1,0:T(8,128)(2,1)S(1)} %get-tuple-element.67), channel_id=1, source_target_pairs={{0,3},{1,2},{2,1},{3,0},{4,7},{5,6},{6,5},{7,4},{8,11},{9,10},{10,... | collective-permute-start | bytes 393224 | tf_op jit(solution)/shard_map/ppermute | solution.py:42
  14.0 5.1 %collective-permute-done.9.refs_2_ = bf16[32,1024]{1,0:T(8,128)(2,1)S(1)} collective-permute-done((bf16[32,1024]{1,0:T(8,128)(2,1)S(1)}, bf16[32,1024]{1,0:T(8,128)(2,1)S(1)}, u32[]{:S(2)}, u32[]{:S(2)}) %collective-permute-start.9) | collective-permute-done | bytes 65568 | tf_op jit(solution)/shard_map/ppermute | solution.py:42
  19.1 0.0 collective-permute-done.10.refs_3_
  19.2 2.0 %collective-permute-start.11 = (bf16[4,32,1024]{2,1,0:T(8,128)(2,1)S(1)}, bf16[4,32,1024]{2,1,0:T(8,128)(2,1)S(1)}, u32[]{:S(2)}, u32[]{:S(2)}) collective-permute-start(bf16[4,32,1024]{2,1,0:T(8,128)(2,1)S(1)} %shard_map.63.refs_0_), channel_id=1, source_target_pairs={{0,8},{4,12},{8,0},{12,4},{1,9},{5,13},{9,1},{13,5},{2,10},{6,14},... | collective-permute-start | bytes 786440 | tf_op jit(solution)/shard_map/ppermute | solution.py:42
  21.2 2.9 %shard_map.55 = (bf16[256,256]{1,0:T(8,128)(2,1)S(1)}, bf16[256,256]{1,0:T(8,128)(2,1)S(1)}, bf16[256,256]{1,0:T(8,128)(2,1)S(1)}, bf16[256,256]{1,0:T(8,128)(2,1)S(1)}) custom-call(bf16[256,1024]{1,0:T(8,128)(2,1)} %x_hbm.3, bf16[1024,2048]{1,0:T(8,128)(2,1)} %w_ref.5), custom_call_target="tpu_custom_call" | custom-call | flops 536870912 | bytes 4718592 | tf_op jit(solution)/shard_map/pallas_call | solution.py:23
  24.1 4.0 %collective-permute-start.2 = (bf16[256,256]{1,0:T(8,128)(2,1)S(1)}, bf16[256,256]{1,0:T(8,128)(2,1)S(1)}, u32[]{:S(2)}, u32[]{:S(2)}) collective-permute-start(bf16[256,256]{1,0:T(8,128)(2,1)S(1)} %get-tuple-element.49), channel_id=1, source_target_pairs={{0,1},{1,0},{2,3},{3,2},{4,5},{5,4},{6,7},{7,6},{8,9},{9,8},{10,11... | collective-permute-start | bytes 393224 | tf_op jit(solution)/shard_map/ppermute | solution.py:42
  28.1 0.0 collective-permute-done.19.rest_0_
  28.1 1.2 %collective-permute-start.1 = (bf16[256,256]{1,0:T(8,128)(2,1)S(1)}, bf16[256,256]{1,0:T(8,128)(2,1)S(1)}, u32[]{:S(2)}, u32[]{:S(2)}) collective-permute-start(bf16[256,256]{1,0:T(8,128)(2,1)S(1)} %get-tuple-element.48), channel_id=1, source_target_pairs={{0,2},{1,3},{2,0},{3,1},{4,6},{5,7},{6,4},{7,5},{8,10},{9,11},{10,... | collective-permute-start | bytes 393224 | tf_op jit(solution)/shard_map/ppermute | solution.py:42
  29.3 1.8 %shard_map.56 = (f32[2,64,2048]{2,1,0:T(8,128)S(1)}, f32[2,2,2048]{2,1,0:T(2,128)S(1)}) custom-call(bf16[4,64,2048]{2,1,0:T(8,128)(2,1)S(1)} %copy-done, bf16[256,256]{1,0:T(8,128)(2,1)S(1)} %get-tuple-element.50.rest_0_), custom_call_target="tpu_custom_call" | custom-call | flops 268435456 | bytes 1179648 | tf_op jit(solution)/shard_map/pallas_call | solution.py:23
  31.1 1.4 %collective-permute-start = (bf16[256,256]{1,0:T(8,128)(2,1)S(1)}, bf16[256,256]{1,0:T(8,128)(2,1)S(1)}, u32[]{:S(2)}, u32[]{:S(2)}) collective-permute-start(bf16[256,256]{1,0:T(8,128)(2,1)S(1)} %get-tuple-element.47), channel_id=1, source_target_pairs={{0,3},{1,2},{2,1},{3,0},{4,7},{5,6},{6,5},{7,4},{8,11},{9,10},{10,... | collective-permute-start | bytes 393224 | tf_op jit(solution)/shard_map/ppermute | solution.py:42
  32.5 1.8 %shard_map.66 = (f32[2,64,2048]{2,1,0:T(8,128)S(1)}, f32[2,2,2048]{2,1,0:T(2,128)S(1)}) custom-call(bf16[4,64,2048]{2,1,0:T(8,128)(2,1)S(1)} %copy-done, bf16[256,256]{1,0:T(8,128)(2,1)S(1)} %get-tuple-element.70.rest_0_), custom_call_target="tpu_custom_call" | custom-call | flops 268435456 | bytes 1179648 | tf_op jit(solution)/shard_map/pallas_call | solution.py:23
  34.3 1.9 %shard_map.67 = (f32[2,64,2048]{2,1,0:T(8,128)S(1)}, f32[2,2,2048]{2,1,0:T(2,128)S(1)}) custom-call(bf16[4,64,2048]{2,1,0:T(8,128)(2,1)S(1)} %copy-done, bf16[256,256]{1,0:T(8,128)(2,1)S(1)} %collective-permute-done.20.rest_0_, f32[2,64,2048]{2,1,0:T(8,128)S(1)} %get-tuple-element.71.rest_1_, f32[2,2,2048]{2,1,0:T(2,128)S(1)} %get-tuple-element.72.rest_2_), custom_call_target="tpu_custom_call" | custom-call | flops 268435456 | bytes 2260992 | tf_op jit(solution)/shard_map/pallas_call | solution.py:23
  36.2 1.9 %shard_map.68 = (f32[2,64,2048]{2,1,0:T(8,128)S(1)}, f32[2,2,2048]{2,1,0:T(2,128)S(1)}) custom-call(bf16[4,64,2048]{2,1,0:T(8,128)(2,1)S(1)} %copy-done, bf16[256,256]{1,0:T(8,128)(2,1)S(1)} %collective-permute-done.19.rest_0_, f32[2,64,2048]{2,1,0:T(8,128)S(1)} %get-tuple-element.73.rest_1_, f32[2,2,2048]{2,1,0:T(2,128)S(1)} %get-tuple-element.74.rest_2_), custom_call_target="tpu_custom_call" | custom-call | flops 268435456 | bytes 2260992 | tf_op jit(solution)/shard_map/pallas_call | solution.py:23
  38.1 2.0 %shard_map.69 = (bf16[2,72,1024]{2,1,0:T(8,128)(2,1)S(1)}, f32[2,64,1024]{2,1,0:T(8,128)S(1)}, f32[2,2,1024]{2,1,0:T(2,128)S(1)}) custom-call(bf16[4,64,2048]{2,1,0:T(8,128)(2,1)S(1)} %copy-done, bf16[256,256]{1,0:T(8,128)(2,1)S(1)} %collective-permute-done.18.rest_0_, f32[2,64,2048]{2,1,0:T(8,128)S(1)} %get-tuple-element.75.rest_1_, ...), custom_call_target="tpu_custom_call" | custom-call | flops 268435456 | bytes 2260992 | tf_op jit(solution)/shard_map/pallas_call | solution.py:23
  40.1 0.1 collective-permute-start.21
  40.1 0.0 collective-permute-done.2.rest_0_
  40.1 1.9 %shard_map.57 = (f32[2,64,2048]{2,1,0:T(8,128)S(1)}, f32[2,2,2048]{2,1,0:T(2,128)S(1)}) custom-call(bf16[4,64,2048]{2,1,0:T(8,128)(2,1)S(1)} %copy-done, bf16[256,256]{1,0:T(8,128)(2,1)S(1)} %collective-permute-done.2.rest_0_, f32[2,64,2048]{2,1,0:T(8,128)S(1)} %get-tuple-element.51.rest_1_, f32[2,2,2048]{2,1,0:T(2,128)S(1)} %get-tuple-element.52.rest_2_), custom_call_target="tpu_custom_call" | custom-call | flops 268435456 | bytes 2260992 | tf_op jit(solution)/shard_map/pallas_call | solution.py:23
  42.0 0.0 collective-permute-done.1.rest_0_
  42.0 2.1 %shard_map.58 = (f32[2,64,2048]{2,1,0:T(8,128)S(1)}, f32[2,2,2048]{2,1,0:T(2,128)S(1)}) custom-call(bf16[4,64,2048]{2,1,0:T(8,128)(2,1)S(1)} %copy-done, bf16[256,256]{1,0:T(8,128)(2,1)S(1)} %collective-permute-done.1.rest_0_, f32[2,64,2048]{2,1,0:T(8,128)S(1)} %get-tuple-element.53.rest_1_, f32[2,2,2048]{2,1,0:T(2,128)S(1)} %get-tuple-element.54.rest_2_), custom_call_target="tpu_custom_call" | custom-call | flops 268435456 | bytes 2260992 | tf_op jit(solution)/shard_map/pallas_call | solution.py:23
  44.1 0.0 collective-permute-done.rest_0_
  44.1 0.0 copy-start.1
  44.1 2.0 %shard_map.59 = (bf16[2,72,1024]{2,1,0:T(8,128)(2,1)S(1)}, f32[2,64,1024]{2,1,0:T(8,128)S(1)}, f32[2,2,1024]{2,1,0:T(2,128)S(1)}) custom-call(bf16[4,64,2048]{2,1,0:T(8,128)(2,1)S(1)} %copy-done, bf16[256,256]{1,0:T(8,128)(2,1)S(1)} %collective-permute-done.rest_0_, f32[2,64,2048]{2,1,0:T(8,128)S(1)} %get-tuple-element.55.rest_1_, ...), custom_call_target="tpu_custom_call" | custom-call | flops 268435456 | bytes 2260992 | tf_op jit(solution)/shard_map/pallas_call | solution.py:23
  46.1 0.6 collective-permute-start.3
  46.7 1.5 %collective-permute-start.12 = (bf16[4,32,1024]{2,1,0:T(8,128)(2,1)S(1)}, bf16[4,32,1024]{2,1,0:T(8,128)(2,1)S(1)}, u32[]{:S(2)}, u32[]{:S(2)}) collective-permute-start(bf16[4,32,1024]{2,1,0:T(8,128)(2,1)S(1)} %shard_map.63.refs_0_), channel_id=1, source_target_pairs={{0,16},{16,0},{1,17},{17,1},{2,18},{18,2},{3,19},{19,3},{4,20},{20... | collective-permute-start | bytes 786440 | tf_op jit(solution)/shard_map/ppermute | solution.py:42
  48.2 0.0 collective-permute-done.11.refs_1_
  48.2 0.5 collective-permute-start.13
  48.7 0.0 collective-permute-done.21.got_ref
  48.7 0.2 shard_map.70
  48.9 0.6 collective-permute-start.22
  49.5 0.0 collective-permute-start.14
  49.5 6.4 %collective-permute-done.12.refs_2_ = bf16[4,32,1024]{2,1,0:T(8,128)(2,1)S(1)} collective-permute-done((bf16[4,32,1024]{2,1,0:T(8,128)(2,1)S(1)}, bf16[4,32,1024]{2,1,0:T(8,128)(2,1)S(1)}, u32[]{:S(2)}, u32[]{:S(2)}) %collective-permute-start.12) | collective-permute-done | bytes 262176 | tf_op jit(solution)/shard_map/ppermute | solution.py:42
  55.8 0.0 collective-permute-start.15
  55.8 0.0 collective-permute-done.3.got_ref
  55.8 0.5 collective-permute-start.16
  56.4 4.2 %collective-permute-done.13.refs_3_ = bf16[4,32,1024]{2,1,0:T(8,128)(2,1)S(1)} collective-permute-done((bf16[4,32,1024]{2,1,0:T(8,128)(2,1)S(1)}, bf16[4,32,1024]{2,1,0:T(8,128)(2,1)S(1)}, u32[]{:S(2)}, u32[]{:S(2)}) %collective-permute-start.13) | collective-permute-done | bytes 262176 | tf_op jit(solution)/shard_map/ppermute | solution.py:42
  60.6 0.2 shard_map.60
  60.7 0.6 collective-permute-start.4
  61.3 0.1 shard_map.71
  61.4 0.0 collective-permute-done.14.refs_4_
  61.4 0.8 collective-permute-start.23
  62.2 4.8 %collective-permute-done.4.got_ref = bf16[2,72,512]{2,1,0:T(8,128)(2,1)S(1)} collective-permute-done((bf16[2,72,512]{2,1,0:T(8,128)(2,1)S(1)}, bf16[2,72,512]{2,1,0:T(8,128)(2,1)S(1)}, u32[]{:S(2)}, u32[]{:S(2)}) %collective-permute-start.4) | collective-permute-done | bytes 147488 | tf_op jit(solution)/shard_map/ppermute | solution.py:42
  67.1 2.0 %collective-permute-start.24 = (bf16[2,64,128]{2,1,0:T(8,128)(2,1)S(1)}, bf16[2,64,128]{2,1,0:T(8,128)(2,1)S(1)}, u32[]{:S(2)}, u32[]{:S(2)}) collective-permute-start(bf16[2,64,128]{2,1,0:T(8,128)(2,1)S(1)} %get-tuple-element.85), channel_id=1, source_target_pairs={{0,2},{1,3},{2,0},{3,1},{4,6},{5,7},{6,4},{7,5},{8,10},{9,11},{10,... | collective-permute-start | bytes 98312 | tf_op jit(solution)/shard_map/ppermute | solution.py:42
  69.1 0.0 collective-permute-done.15.refs_5_
  69.1 1.3 %collective-permute-start.25 = (bf16[2,64,128]{2,1,0:T(8,128)(2,1)S(1)}, bf16[2,64,128]{2,1,0:T(8,128)(2,1)S(1)}, u32[]{:S(2)}, u32[]{:S(2)}) collective-permute-start(bf16[2,64,128]{2,1,0:T(8,128)(2,1)S(1)} %get-tuple-element.86), channel_id=1, source_target_pairs={{0,3},{1,2},{2,1},{3,0},{4,7},{5,6},{6,5},{7,4},{8,11},{9,10},{10,... | collective-permute-start | bytes 98312 | tf_op jit(solution)/shard_map/ppermute | solution.py:42
  70.4 0.1 shard_map.61
  70.5 0.2 collective-permute-start.5
  70.7 0.0 collective-permute-done.23.refs_1_
  70.7 2.9 %collective-permute-start.6 = (bf16[2,64,128]{2,1,0:T(8,128)(2,1)S(1)}, bf16[2,64,128]{2,1,0:T(8,128)(2,1)S(1)}, u32[]{:S(2)}, u32[]{:S(2)}) collective-permute-start(bf16[2,64,128]{2,1,0:T(8,128)(2,1)S(1)} %get-tuple-element.65), channel_id=1, source_target_pairs={{0,2},{1,3},{2,0},{3,1},{4,6},{5,7},{6,4},{7,5},{8,10},{9,11},{10,... | collective-permute-start | bytes 98312 | tf_op jit(solution)/shard_map/ppermute | solution.py:42
  73.7 1.3 %collective-permute-start.7 = (bf16[2,64,128]{2,1,0:T(8,128)(2,1)S(1)}, bf16[2,64,128]{2,1,0:T(8,128)(2,1)S(1)}, u32[]{:S(2)}, u32[]{:S(2)}) collective-permute-start(bf16[2,64,128]{2,1,0:T(8,128)(2,1)S(1)} %get-tuple-element.66), channel_id=1, source_target_pairs={{0,3},{1,2},{2,1},{3,0},{4,7},{5,6},{6,5},{7,4},{8,11},{9,10},{10,... | collective-permute-start | bytes 98312 | tf_op jit(solution)/shard_map/ppermute | solution.py:42
  74.9 0.2 shard_map.64.refs_5_
  75.1 0.0 collective-permute-done.24.refs_2_
  75.1 0.5 shard_map.72
  75.6 0.0 collective-permute-done.5.refs_1_
  75.6 0.1 collective-permute-done.6.refs_2_
  75.7 3.7 %collective-permute-done.7.refs_3_ = bf16[2,64,128]{2,1,0:T(8,128)(2,1)S(1)} collective-permute-done((bf16[2,64,128]{2,1,0:T(8,128)(2,1)S(1)}, bf16[2,64,128]{2,1,0:T(8,128)(2,1)S(1)}, u32[]{:S(2)}, u32[]{:S(2)}) %collective-permute-start.7) | collective-permute-done | bytes 32800 | tf_op jit(solution)/shard_map/ppermute | solution.py:42
  79.4 1.2 %shard_map.73 = bf16[128,1024]{1,0:T(8,128)(2,1)} custom-call(bf16[2,64,128]{2,1,0:T(8,128)(2,1)S(1)} %get-tuple-element.63.refs_0_, bf16[2,64,128]{2,1,0:T(8,128)(2,1)S(1)} %collective-permute-done.5.refs_1_, bf16[2,64,128]{2,1,0:T(8,128)(2,1)S(1)} %collective-permute-done.6.refs_2_, bf16[2,64,128]{2,1,0:T(8,128)(2,1)S(1)} %collective-permute-done.7.refs_3_, ...), custom_call_target="tpu_custom_call" | custom-call | flops 134217728 | bytes 2757120 | tf_op jit(solution)/shard_map/pallas_call | solution.py:23
  (11 shorter events, 0.0 us)
Async XLA Ops:
  0.0 29.3 %copy-start = (bf16[4,64,2048]{2,1,0:T(8,128)(2,1)S(1)}, bf16[4,64,2048]{2,1,0:T(8,128)(2,1)}, u32[]{:S(2)}) copy-start(bf16[4,64,2048]{2,1,0:T(8,128)(2,1)} %q_ref.15) | copy-start | bytes 3145732
  3.0 25.1 %collective-permute-start.19 = (bf16[256,256]{1,0:T(8,128)(2,1)S(1)}, bf16[256,256]{1,0:T(8,128)(2,1)S(1)}, u32[]{:S(2)}, u32[]{:S(2)}) collective-permute-start(bf16[256,256]{1,0:T(8,128)(2,1)S(1)} %get-tuple-element.68), channel_id=1, source_target_pairs={{0,2},{1,3},{2,0},{3,1},{4,6},{5,7},{6,4},{7,5},{8,10},{9,11},{10,... | collective-permute-start | bytes 393224 | tf_op jit(solution)/shard_map/ppermute | solution.py:42
  8.0 5.1 %collective-permute-start.8 = (bf16[32,1024]{1,0:T(8,128)(2,1)S(1)}, bf16[32,1024]{1,0:T(8,128)(2,1)S(1)}, u32[]{:S(2)}, u32[]{:S(2)}) collective-permute-start(bf16[32,1024]{1,0:T(8,128)(2,1)S(1)} %shard_map.62.refs_0_), channel_id=1, source_target_pairs={{0,1},{1,0},{2,3},{3,2},{4,5},{5,4},{6,7},{7,6},{8,9},{9,8},{10,11... | collective-permute-start | bytes 196616 | tf_op jit(solution)/shard_map/ppermute | solution.py:42
  9.7 9.5 %collective-permute-start.9 = (bf16[32,1024]{1,0:T(8,128)(2,1)S(1)}, bf16[32,1024]{1,0:T(8,128)(2,1)S(1)}, u32[]{:S(2)}, u32[]{:S(2)}) collective-permute-start(bf16[32,1024]{1,0:T(8,128)(2,1)S(1)} %shard_map.62.refs_0_), channel_id=1, source_target_pairs={{0,2},{1,3},{2,0},{3,1},{4,6},{5,7},{6,4},{7,5},{8,10},{9,11},{10,... | collective-permute-start | bytes 196616 | tf_op jit(solution)/shard_map/ppermute | solution.py:42
  10.0 9.1 %collective-permute-start.10 = (bf16[32,1024]{1,0:T(8,128)(2,1)S(1)}, bf16[32,1024]{1,0:T(8,128)(2,1)S(1)}, u32[]{:S(2)}, u32[]{:S(2)}) collective-permute-start(bf16[32,1024]{1,0:T(8,128)(2,1)S(1)} %shard_map.62.refs_0_), channel_id=1, source_target_pairs={{0,3},{1,2},{2,1},{3,0},{4,7},{5,6},{6,5},{7,4},{8,11},{9,10},{10,... | collective-permute-start | bytes 196616 | tf_op jit(solution)/shard_map/ppermute | solution.py:42
  12.5 18.6 %collective-permute-start.20 = (bf16[256,256]{1,0:T(8,128)(2,1)S(1)}, bf16[256,256]{1,0:T(8,128)(2,1)S(1)}, u32[]{:S(2)}, u32[]{:S(2)}) collective-permute-start(bf16[256,256]{1,0:T(8,128)(2,1)S(1)} %get-tuple-element.69), channel_id=1, source_target_pairs={{0,1},{1,0},{2,3},{3,2},{4,5},{5,4},{6,7},{7,6},{8,9},{9,8},{10,11... | collective-permute-start | bytes 393224 | tf_op jit(solution)/shard_map/ppermute | solution.py:42
  13.1 24.9 %collective-permute-start.18 = (bf16[256,256]{1,0:T(8,128)(2,1)S(1)}, bf16[256,256]{1,0:T(8,128)(2,1)S(1)}, u32[]{:S(2)}, u32[]{:S(2)}) collective-permute-start(bf16[256,256]{1,0:T(8,128)(2,1)S(1)} %get-tuple-element.67), channel_id=1, source_target_pairs={{0,3},{1,2},{2,1},{3,0},{4,7},{5,6},{6,5},{7,4},{8,11},{9,10},{10,... | collective-permute-start | bytes 393224 | tf_op jit(solution)/shard_map/ppermute | solution.py:42
  19.2 29.0 %collective-permute-start.11 = (bf16[4,32,1024]{2,1,0:T(8,128)(2,1)S(1)}, bf16[4,32,1024]{2,1,0:T(8,128)(2,1)S(1)}, u32[]{:S(2)}, u32[]{:S(2)}) collective-permute-start(bf16[4,32,1024]{2,1,0:T(8,128)(2,1)S(1)} %shard_map.63.refs_0_), channel_id=1, source_target_pairs={{0,8},{4,12},{8,0},{12,4},{1,9},{5,13},{9,1},{13,5},{2,10},{6,14},... | collective-permute-start | bytes 786440 | tf_op jit(solution)/shard_map/ppermute | solution.py:42
  24.1 16.0 %collective-permute-start.2 = (bf16[256,256]{1,0:T(8,128)(2,1)S(1)}, bf16[256,256]{1,0:T(8,128)(2,1)S(1)}, u32[]{:S(2)}, u32[]{:S(2)}) collective-permute-start(bf16[256,256]{1,0:T(8,128)(2,1)S(1)} %get-tuple-element.49), channel_id=1, source_target_pairs={{0,1},{1,0},{2,3},{3,2},{4,5},{5,4},{6,7},{7,6},{8,9},{9,8},{10,11... | collective-permute-start | bytes 393224 | tf_op jit(solution)/shard_map/ppermute | solution.py:42
  28.1 13.9 %collective-permute-start.1 = (bf16[256,256]{1,0:T(8,128)(2,1)S(1)}, bf16[256,256]{1,0:T(8,128)(2,1)S(1)}, u32[]{:S(2)}, u32[]{:S(2)}) collective-permute-start(bf16[256,256]{1,0:T(8,128)(2,1)S(1)} %get-tuple-element.48), channel_id=1, source_target_pairs={{0,2},{1,3},{2,0},{3,1},{4,6},{5,7},{6,4},{7,5},{8,10},{9,11},{10,... | collective-permute-start | bytes 393224 | tf_op jit(solution)/shard_map/ppermute | solution.py:42
  31.1 13.0 %collective-permute-start = (bf16[256,256]{1,0:T(8,128)(2,1)S(1)}, bf16[256,256]{1,0:T(8,128)(2,1)S(1)}, u32[]{:S(2)}, u32[]{:S(2)}) collective-permute-start(bf16[256,256]{1,0:T(8,128)(2,1)S(1)} %get-tuple-element.47), channel_id=1, source_target_pairs={{0,3},{1,2},{2,1},{3,0},{4,7},{5,6},{6,5},{7,4},{8,11},{9,10},{10,... | collective-permute-start | bytes 393224 | tf_op jit(solution)/shard_map/ppermute | solution.py:42
  40.1 8.6 %collective-permute-start.21 = (bf16[2,72,1024]{2,1,0:T(8,128)(2,1)S(1)}, bf16[2,72,1024]{2,1,0:T(8,128)(2,1)S(1)}, u32[]{:S(2)}, u32[]{:S(2)}) collective-permute-start(bf16[2,72,1024]{2,1,0:T(8,128)(2,1)S(1)} %get-tuple-element.77), channel_id=1, source_target_pairs={{0,4},{4,0},{8,12},{12,8},{1,5},{5,1},{9,13},{13,9},{2,6},{6,2},{1... | collective-permute-start | bytes 884744 | tf_op jit(solution)/shard_map/ppermute | solution.py:42
  44.1 31.0 %copy-start.1 = (f32[1024]{0:T(1024)S(1)}, f32[1024]{0:T(1024)}, u32[]{:S(2)}) copy-start(f32[1024]{0:T(1024)} %param.8) | copy-start | bytes 12292
  46.1 9.7 %collective-permute-start.3 = (bf16[2,72,1024]{2,1,0:T(8,128)(2,1)S(1)}, bf16[2,72,1024]{2,1,0:T(8,128)(2,1)S(1)}, u32[]{:S(2)}, u32[]{:S(2)}) collective-permute-start(bf16[2,72,1024]{2,1,0:T(8,128)(2,1)S(1)} %get-tuple-element.57), channel_id=1, source_target_pairs={{0,4},{4,0},{8,12},{12,8},{1,5},{5,1},{9,13},{13,9},{2,6},{6,2},{1... | collective-permute-start | bytes 884744 | tf_op jit(solution)/shard_map/ppermute | solution.py:42
  46.7 9.2 %collective-permute-start.12 = (bf16[4,32,1024]{2,1,0:T(8,128)(2,1)S(1)}, bf16[4,32,1024]{2,1,0:T(8,128)(2,1)S(1)}, u32[]{:S(2)}, u32[]{:S(2)}) collective-permute-start(bf16[4,32,1024]{2,1,0:T(8,128)(2,1)S(1)} %shard_map.63.refs_0_), channel_id=1, source_target_pairs={{0,16},{16,0},{1,17},{17,1},{2,18},{18,2},{3,19},{19,3},{4,20},{20... | collective-permute-start | bytes 786440 | tf_op jit(solution)/shard_map/ppermute | solution.py:42
  48.2 12.4 %collective-permute-start.13 = (bf16[4,32,1024]{2,1,0:T(8,128)(2,1)S(1)}, bf16[4,32,1024]{2,1,0:T(8,128)(2,1)S(1)}, u32[]{:S(2)}, u32[]{:S(2)}) collective-permute-start(bf16[4,32,1024]{2,1,0:T(8,128)(2,1)S(1)} %collective-permute-done.11.refs_1_), channel_id=1, source_target_pairs={{0,16},{16,0},{1,17},{17,1},{2,18},{18,2},{3,19},{19,3},{4,20},{20... | collective-permute-start | bytes 786440 | tf_op jit(solution)/shard_map/ppermute | solution.py:42
  48.9 11.9 %collective-permute-start.22 = (bf16[2,72,512]{2,1,0:T(8,128)(2,1)S(1)}, bf16[2,72,512]{2,1,0:T(8,128)(2,1)S(1)}, u32[]{:S(2)}, u32[]{:S(2)}) collective-permute-start(bf16[2,72,512]{2,1,0:T(8,128)(2,1)S(1)} %get-tuple-element.80), channel_id=1, source_target_pairs={{0,8},{4,12},{8,0},{12,4},{1,9},{5,13},{9,1},{13,5},{2,10},{6,14},... | collective-permute-start | bytes 442376 | tf_op jit(solution)/shard_map/ppermute | solution.py:42
  49.5 12.0 %collective-permute-start.14 = (bf16[4,32,1024]{2,1,0:T(8,128)(2,1)S(1)}, bf16[4,32,1024]{2,1,0:T(8,128)(2,1)S(1)}, u32[]{:S(2)}, u32[]{:S(2)}) collective-permute-start(bf16[4,32,1024]{2,1,0:T(8,128)(2,1)S(1)} %shard_map.63.refs_0_), channel_id=1, source_target_pairs={{0,4},{4,0},{8,12},{12,8},{1,5},{5,1},{9,13},{13,9},{2,6},{6,2},{1... | collective-permute-start | bytes 786440 | tf_op jit(solution)/shard_map/ppermute | solution.py:42
  55.8 13.3 %collective-permute-start.15 = (bf16[4,32,1024]{2,1,0:T(8,128)(2,1)S(1)}, bf16[4,32,1024]{2,1,0:T(8,128)(2,1)S(1)}, u32[]{:S(2)}, u32[]{:S(2)}) collective-permute-start(bf16[4,32,1024]{2,1,0:T(8,128)(2,1)S(1)} %collective-permute-done.11.refs_1_), channel_id=1, source_target_pairs={{0,4},{4,0},{8,12},{12,8},{1,5},{5,1},{9,13},{13,9},{2,6},{6,2},{1... | collective-permute-start | bytes 786440 | tf_op jit(solution)/shard_map/ppermute | solution.py:42
  55.8 14.6 %collective-permute-start.16 = (bf16[4,32,1024]{2,1,0:T(8,128)(2,1)S(1)}, bf16[4,32,1024]{2,1,0:T(8,128)(2,1)S(1)}, u32[]{:S(2)}, u32[]{:S(2)}) collective-permute-start(bf16[4,32,1024]{2,1,0:T(8,128)(2,1)S(1)} %collective-permute-done.12.refs_2_), channel_id=1, source_target_pairs={{0,4},{4,0},{8,12},{12,8},{1,5},{5,1},{9,13},{13,9},{2,6},{6,2},{1... | collective-permute-start | bytes 786440 | tf_op jit(solution)/shard_map/ppermute | solution.py:42
  60.6 13.1 %collective-permute-start.17 = (bf16[4,32,1024]{2,1,0:T(8,128)(2,1)S(1)}, bf16[4,32,1024]{2,1,0:T(8,128)(2,1)S(1)}, u32[]{:S(2)}, u32[]{:S(2)}) collective-permute-start(bf16[4,32,1024]{2,1,0:T(8,128)(2,1)S(1)} %collective-permute-done.13.refs_3_), channel_id=1, source_target_pairs={{0,4},{4,0},{8,12},{12,8},{1,5},{5,1},{9,13},{13,9},{2,6},{6,2},{1... | collective-permute-start | bytes 786440 | tf_op jit(solution)/shard_map/ppermute | solution.py:42
  60.7 6.3 %collective-permute-start.4 = (bf16[2,72,512]{2,1,0:T(8,128)(2,1)S(1)}, bf16[2,72,512]{2,1,0:T(8,128)(2,1)S(1)}, u32[]{:S(2)}, u32[]{:S(2)}) collective-permute-start(bf16[2,72,512]{2,1,0:T(8,128)(2,1)S(1)} %get-tuple-element.60), channel_id=1, source_target_pairs={{0,8},{4,12},{8,0},{12,4},{1,9},{5,13},{9,1},{13,5},{2,10},{6,14},... | collective-permute-start | bytes 442376 | tf_op jit(solution)/shard_map/ppermute | solution.py:42
  61.4 9.3 %collective-permute-start.23 = (bf16[2,64,128]{2,1,0:T(8,128)(2,1)S(1)}, bf16[2,64,128]{2,1,0:T(8,128)(2,1)S(1)}, u32[]{:S(2)}, u32[]{:S(2)}) collective-permute-start(bf16[2,64,128]{2,1,0:T(8,128)(2,1)S(1)} %get-tuple-element.84), channel_id=1, source_target_pairs={{0,1},{1,0},{2,3},{3,2},{4,5},{5,4},{6,7},{7,6},{8,9},{9,8},{10,11... | collective-permute-start | bytes 98312 | tf_op jit(solution)/shard_map/ppermute | solution.py:42
  67.1 8.0 %collective-permute-start.24 = (bf16[2,64,128]{2,1,0:T(8,128)(2,1)S(1)}, bf16[2,64,128]{2,1,0:T(8,128)(2,1)S(1)}, u32[]{:S(2)}, u32[]{:S(2)}) collective-permute-start(bf16[2,64,128]{2,1,0:T(8,128)(2,1)S(1)} %get-tuple-element.85), channel_id=1, source_target_pairs={{0,2},{1,3},{2,0},{3,1},{4,6},{5,7},{6,4},{7,5},{8,10},{9,11},{10,... | collective-permute-start | bytes 98312 | tf_op jit(solution)/shard_map/ppermute | solution.py:42
  69.1 6.0 %collective-permute-start.25 = (bf16[2,64,128]{2,1,0:T(8,128)(2,1)S(1)}, bf16[2,64,128]{2,1,0:T(8,128)(2,1)S(1)}, u32[]{:S(2)}, u32[]{:S(2)}) collective-permute-start(bf16[2,64,128]{2,1,0:T(8,128)(2,1)S(1)} %get-tuple-element.86), channel_id=1, source_target_pairs={{0,3},{1,2},{2,1},{3,0},{4,7},{5,6},{6,5},{7,4},{8,11},{9,10},{10,... | collective-permute-start | bytes 98312 | tf_op jit(solution)/shard_map/ppermute | solution.py:42
  70.5 5.1 %collective-permute-start.5 = (bf16[2,64,128]{2,1,0:T(8,128)(2,1)S(1)}, bf16[2,64,128]{2,1,0:T(8,128)(2,1)S(1)}, u32[]{:S(2)}, u32[]{:S(2)}) collective-permute-start(bf16[2,64,128]{2,1,0:T(8,128)(2,1)S(1)} %get-tuple-element.64), channel_id=1, source_target_pairs={{0,1},{1,0},{2,3},{3,2},{4,5},{5,4},{6,7},{7,6},{8,9},{9,8},{10,11... | collective-permute-start | bytes 98312 | tf_op jit(solution)/shard_map/ppermute | solution.py:42
  70.7 5.0 %collective-permute-start.6 = (bf16[2,64,128]{2,1,0:T(8,128)(2,1)S(1)}, bf16[2,64,128]{2,1,0:T(8,128)(2,1)S(1)}, u32[]{:S(2)}, u32[]{:S(2)}) collective-permute-start(bf16[2,64,128]{2,1,0:T(8,128)(2,1)S(1)} %get-tuple-element.65), channel_id=1, source_target_pairs={{0,2},{1,3},{2,0},{3,1},{4,6},{5,7},{6,4},{7,5},{8,10},{9,11},{10,... | collective-permute-start | bytes 98312 | tf_op jit(solution)/shard_map/ppermute | solution.py:42
  73.7 5.7 %collective-permute-start.7 = (bf16[2,64,128]{2,1,0:T(8,128)(2,1)S(1)}, bf16[2,64,128]{2,1,0:T(8,128)(2,1)S(1)}, u32[]{:S(2)}, u32[]{:S(2)}) collective-permute-start(bf16[2,64,128]{2,1,0:T(8,128)(2,1)S(1)} %get-tuple-element.66), channel_id=1, source_target_pairs={{0,3},{1,2},{2,1},{3,0},{4,7},{5,6},{6,5},{7,4},{8,11},{9,10},{10,... | collective-permute-start | bytes 98312 | tf_op jit(solution)/shard_map/ppermute | solution.py:42

commit v3 on v2

--- a/solution.py
+++ b/solution.py
@@ -42,51 +42,91 @@
     return lax.ppermute(value, axis, [(i, i ^ step) for i in range(count)])
 
 
-def project_kernel(total, offset, width, size, scale, x_hbm, w_ref, *rest):
-    count = lax.axis_size("head")
-    outs, (x_ref, slots, x_sem, sems) = rest[:count], rest[count:]
+def project_kernel(plan, total, size, scale, piece, *refs):
     here = lax.axis_index("head")
-    fetch = pltpu.make_async_copy(x_hbm, x_ref, x_sem)
-    fetch.start()
+    x_in, w_in, refs = refs[0], refs[1], refs[2:]
+    if piece:
+        o_in, refs = refs[0], refs[1:]
+    outs, refs = refs[: len(plan)], refs[len(plan) :]
     copies = []
-    order = list(range(count - 1, -1, -1))
-    for step in order:
-        first = (here ^ step) * total + offset
-        columns = pl.ds(pl.multiple_of(first, 128), width)
-        copy = pltpu.make_async_copy(w_ref.at[:, columns], slots.at[step], sems.at[step])
+    if piece:
+        (x_ref, own_ref, slots, sems, sem), at = refs, None
+        place = lax.axis_index("groups") * lax.axis_size("ctx") + lax.axis_index("ctx")
+        mine = pl.ds(pl.multiple_of(place * piece, piece), piece)
+        fetch = pltpu.make_async_copy(x_in, x_ref, sem.at[0])
+        fetch.start()
+        carry = pltpu.make_async_copy(o_in.at[mine, :], own_ref, sem.at[1])
+    else:
+        x_ref, (slots, sems) = x_in, refs
+    at = 0
+    for n, (step, first, heads, _) in enumerate(plan):
+        width = 2 * size * heads
+        start = (here ^ step) * total + 2 * size * first
+        columns = pl.ds(pl.multiple_of(start, 128), width)
+        copy = pltpu.make_async_copy(
+            w_in.at[:, columns], slots.at[:, at : at + width], sems.at[n]
+        )
         copy.start()
-        copies.append(copy)
-    column = lax.broadcasted_iota(jnp.int32, (1, width), 1)
-    factor = jnp.where(lax.rem(column, 2 * size) < size, scale, 1.0).astype(f32)
-    fetch.wait()
-    for copy, step in zip(copies, order):
+        copies.append((copy, at, width))
+        at += width
+    if piece:
+        carry.start()
+        fetch.wait()
+    rows = x_ref.shape[0]
+    for (copy, at, width), (_, _, _, carries), out_ref in zip(copies, plan, outs):
+        column = lax.broadcasted_iota(jnp.int32, (1, width), 1)
+        factor = jnp.where(lax.rem(column, 2 * size) < size, scale, 1.0).astype(f32)
         copy.wait()
-        product = jnp.dot(x_ref[...], slots[step], preferred_element_type=f32)
-        outs[step][...] = (product * factor).astype(bf16)
-
-
-def project(context, w_kv, offset, heads, size):
-    count = lax.axis_size("head")
+        product = jnp.dot(x_ref[...], slots[:, at : at + width], preferred_element_type=f32)
+        out_ref[0:rows, :] = (product * factor).astype(bf16)
+    if piece:
+        carry.wait()
+        for (_, _, width), (_, _, _, carries), out_ref in zip(copies, plan, outs):
+            if carries:
+                for j, at in enumerate(range(0, own_ref.shape[1], width)):
+                    part = own_ref[:, at : at + width]
+                    below = slice(rows + j * piece, rows + (j + 1) * piece)
+                    out_ref[below, 0 : part.shape[1]] = part
+
+
+def carry_kernel(x_ref, own_ref, out_ref):
+    rows, width = x_ref.shape
+    piece = own_ref.shape[0]
+    out_ref[0:rows, :] = x_ref[...]
+    for j, at in enumerate(range(0, own_ref.shape[1], width)):
+        part = own_ref[:, at : at + width]
+        below = slice(rows + j * piece, rows + (j + 1) * piece)
+        out_ref[below, 0 : part.shape[1]] = part
+
+
+def project(context, w_kv, w_out, plan, size, pieces):
     rows, depth = context.shape
-    width = 2 * size * heads
-    total = w_kv.shape[1] // count
+    heads = sum(p[2] for p in plan)
+    total = w_kv.shape[1] // lax.axis_size("head")
+    piece = w_out.shape[0] // pieces if w_out is not None else 0
+    out_shape = []
+    for _, _, n, carries in plan:
+        width = 2 * size * n
+        extra = piece * (-(-w_out.shape[1] // width)) if carries else 0
+        out_shape.append(shape((rows + extra, width), bf16))
+    scratch = [
+        pltpu.VMEM((depth, 2 * size * heads), bf16),
+        pltpu.SemaphoreType.DMA((len(plan),)),
+    ]
+    far = functools.partial(pltpu.with_memory_space_constraint, memory_space=pltpu.HBM)
+    if piece:
+        args, specs = [far(context), far(w_kv), far(w_out)], [in_hbm] * 3
+        out_shape += [shape(context.shape, bf16), shape((piece, w_out.shape[1]), bf16)]
+        scratch.append(pltpu.SemaphoreType.DMA((2,)))
+    else:
+        args, specs = [context, far(w_kv)], [vmem, in_hbm]
     return call(
-        functools.partial(
-            project_kernel, total, 2 * size * offset, width, size, 1.0 / math.sqrt(size)
-        ),
-        [shape((rows, width), bf16)] * count,
-        [
-            pltpu.with_memory_space_constraint(context, pltpu.HBM),
-            pltpu.with_memory_space_constraint(w_kv, pltpu.HBM),
-        ],
-        flops=2 * rows * depth * width * count,
-        scratch=[
-            pltpu.VMEM((rows, depth), bf16),
-            pltpu.VMEM((count, depth, width), bf16),
-            pltpu.SemaphoreType.DMA,
-            pltpu.SemaphoreType.DMA((count,)),
-        ],
-        in_specs=[in_hbm, in_hbm],
+        functools.partial(project_kernel, plan, total, size, 1.0 / math.sqrt(size), piece),
+        out_shape,
+        args,
+        flops=4 * rows * depth * size * heads,
+        scratch=scratch,
+        in_specs=specs,
     )
 
 
@@ -107,6 +147,7 @@
 
 
 def attend_kernel(offset, rows, sources, tile, first, last, q_ref, *rest):
+    base = 0 if not last else offset
     kv_refs, rest = rest[:sources], rest[sources:]
     if not first:
         (old_ref, old_stat_ref), rest = rest[:2], rest[2:]
@@ -143,7 +184,7 @@
                 r[0:rows, at + size : at + 2 * size].astype(f32).T.astype(bf16) for r in kv_refs
             ]
         query = q_ref[offset + head, :, lanes_of(item)]
-        top = None if first else old_stat_ref[head, 0:1, lanes_of(item)]
+        top = None if first else old_stat_ref[base + head, 0:1, lanes_of(item)]
         for i in range(sources):
             s = jnp.dot(keys[head][i], query, preferred_element_type=f32)
             scores_ref[slot, i] = s
@@ -157,9 +198,9 @@
         if first:
             total, summed = 0.0, 0.0
         else:
-            fade = jnp.exp(old_stat_ref[head, 0:1, lanes] - top)
-            total = old_stat_ref[head, 1:2, lanes] * fade
-            summed = old_ref[head, :, lanes] * fade
+            fade = jnp.exp(old_stat_ref[base + head, 0:1, lanes] - top)
+            total = old_stat_ref[base + head, 1:2, lanes] * fade
+            summed = old_ref[base + head, :, lanes] * fade
         for i in range(sources):
             weights = jnp.exp(scores_ref[slot, i] - top)
             total += jnp.sum(weights, axis=0, keepdims=True)
@@ -268,17 +309,18 @@
     )
 
 
-def pick_kernel(piece, w_ref, out_ref, sem):
-    place = lax.axis_index("groups") * lax.axis_size("ctx") + lax.axis_index("ctx")
-    rows = pl.ds(pl.multiple_of(place * piece, piece), piece)
-    copy = pltpu.make_async_copy(w_ref.at[rows, :], out_ref, sem)
-    copy.start()
-    copy.wait()
-
-
-def stack_kernel(*refs):
-    for n, ref in enumerate(refs[:-1]):
-        refs[-1][n] = ref[...]
+def stack_kernel(context_rows, *refs):
+    out_ref = refs[-1]
+    _, piece, columns = out_ref.shape
+    for step, ref in enumerate(refs[:-1]):
+        rows, width = ref.shape
+        if rows == piece:
+            out_ref[step] = ref[...]
+            continue
+        for j, at in enumerate(range(0, columns, width)):
+            wide = min(width, columns - at)
+            here = slice(context_rows + j * piece, context_rows + (j + 1) * piece)
+            out_ref[step, :, at : at + wide] = ref[here, 0:wide]
 
 
 def order_kernel(offsets, *refs):
@@ -290,18 +332,16 @@
         out_ref[:, pl.ds(start, piece), :] = ref[...]
 
 
-def gather_w_out(w_out, pieces):
-    heads, (rows, columns) = lax.axis_size("head"), w_out.shape
+def gather_w_out(parts, context_rows, w_out, pieces):
+    heads, (rows, columns) = len(parts), w_out.shape
     piece = rows // pieces
-    (own,) = call(
-        functools.partial(pick_kernel, piece),
-        [shape((piece, columns), bf16)],
-        [pltpu.with_memory_space_constraint(w_out, pltpu.HBM)],
-        scratch=[pltpu.SemaphoreType.DMA],
-        in_specs=[in_hbm],
-    )
-    moved = [partner(own, "head", s) for s in range(1, heads)]
-    held = list(call(stack_kernel, [shape((heads, piece, columns), bf16)], [own] + moved))
+    held = list(
+        call(
+            functools.partial(stack_kernel, context_rows),
+            [shape((heads, piece, columns), bf16)],
+            parts,
+        )
+    )
     ctx = lax.axis_size("ctx")
     steps = [("ctx", 1 << b, 1 << b) for b in range(1, (ctx - 1).bit_length())]
     steps += [
@@ -456,37 +496,48 @@
 
 
 def fast_body(context, w_kv, queries, gain, w_out):
-    _, size, _ = queries.shape
+    heads_local, size, _ = queries.shape
     rows = context.shape[0]
     head_count = lax.axis_size("head")
     ctx_count = lax.axis_size("ctx")
     pieces = ctx_count * lax.axis_size("groups")
-    chunk_heads = CHUNKS
-    starts = [sum(chunk_heads[:n]) for n in range(len(chunk_heads))]
-
-    received = []
-    for n, heads in enumerate(chunk_heads):
-        parts = project(context, w_kv, starts[n], heads, size)
-        moved = [partner(parts[s], "head", s) for s in range(head_count - 1, 0, -1)][::-1]
-        received.append([parts[0]] + moved)
-    w_full = gather_w_out(w_out, pieces)
+    starts = [sum(CHUNKS[:n]) for n in range(len(CHUNKS))]
+    final = head_count // 2
+    far = head_count - 1
+
+    part, near, own = project(context, w_kv, w_out, [(far, 0, heads_local, True)], size, pieces)
+    moved = {far: partner(part, "head", far)}
+    others = [s for s in range(far) if s != final]
+    plan = [(s, 0, heads_local, False) for s in others[::-1]]
+    plan += [(final, first, n, False) for first, n in zip(starts, CHUNKS)]
+    parts = project(near, w_kv, None, plan, size, pieces)
+    for s, part in zip(others[::-1], parts):
+        if s:
+            extra = own.shape[0] * own.shape[1] // part.shape[1]
+            (part,) = call(carry_kernel, [shape((rows + extra, part.shape[1]), bf16)], [part, own])
+        moved[s] = partner(part, "head", s) if s else part
+    late = [partner(p, "head", final) for p in parts[len(others) :]]
+    riders = [
+        own if s == 0 else partner(own, "head", s) if s == final else moved[s]
+        for s in range(head_count)
+    ]
+    w_full = gather_w_out(riders, rows, w_out, pieces)
+    state = None
+    for s in others + [far]:
+        state = attend(queries, [moved[s]], state, rows, 0, False)
 
     finished = []
-    for n in range(len(chunk_heads)):
-        state = None
-        for s in range(head_count):
-            state = attend(queries, [received[n][s]], state, rows, starts[n], s == head_count - 1)
+    for n in range(len(CHUNKS)):
+        sums = attend(queries, [late[n]], state, rows, starts[n], True)
         level = 0
         while (ctx_count >> level) > 1:
-            got = partner(state[0], "ctx", 1 << level)
+            got = partner(sums[0], "ctx", 1 << level)
             level += 1
-            state = merge(level, got, *state[1:])
-        finished.append(
-            [partner(state[s], "head", s) if s else state[s] for s in range(head_count)]
-        )
+            sums = merge(level, got, *sums[1:])
+        finished.append([partner(sums[s], "head", s) if s else sums[s] for s in range(head_count)])
     state = None
-    for n in range(len(chunk_heads)):
-        last = n + 1 == len(chunk_heads)
+    for n in range(len(CHUNKS)):
+        last = n + 1 == len(CHUNKS)
         state = output(finished[n], state, starts[n], gain, w_full, last)
     return state[0]
 

time: 80.7 us -> 80.7 us (level)
  waiting for transfers between devices: 24.3 us -> 36.5 us
  starting transfers between devices: 31.7 us -> 22.1 us
  Pallas kernels: 24.3 us -> 21.8 us
    ppermute x26 -> x22, waiting for transfers between devices: 24.3 us -> 36.5 us  [partner(): return lax.ppermute(value, axis, [(i, i ^ step) for i in range(count)])]
    ppermute x26 -> x22, starting transfers between devices: 31.7 us -> 22.1 us  [partner(): return lax.ppermute(value, axis, [(i, i ^ step) for i in range(count)])]
    pallas_call x19 -> x16, Pallas kernels: 24.3 us -> 21.8 us  [call(): pl.pallas_call(kernel, out_shape=out_shape, in_specs=in_specs or [vmem] *...]
  transfers between devices with their start and end apart: 26 -> 22, of which waited for: 6 -> 6; matrix products, arithmetic and copies ran while one was open for 0% -> 0% of each run, Pallas kernels for 25% -> 19%
where the time goes in v3:
time: 80.7 us; the launch traced here: 80.6 us
  waiting for transfers between devices  36.5 us (45%)
  starting transfers between devices  22.1 us (27%)
  Pallas kernels  21.8 us (27%)
    ppermute x22, waiting for transfers between devices, partner(): return lax.ppermute(value, axis, [(i, i ^ step) for i in range(count)])  36.5 us
    ppermute x22, starting transfers between devices, partner(): return lax.ppermute(value, axis, [(i, i ^ step) for i in range(count)])  22.1 us
    pallas_call x16, Pallas kernels, call(): pl.pallas_call(kernel, out_shape=out_shape, in_specs=in_specs or [vmem] *...  21.8 us
  transfers between devices with their start and end apart: 22, of which 6 were waited for; matrix products, arithmetic and copies ran while one was open for 0% of the time, Pallas kernels for 19%

profile of v3, /device:TPU:0, one launch (start us, length us, event | category | flops | bytes accessed | tf_op | source)
XLA Modules:
  0.0 80.6 jit_solution(6024945339015002651)
XLA Ops:
  0.0 1.9 %shard_map.55 = (bf16[320,512]{1,0:T(8,128)(2,1)S(1)}, bf16[256,1024]{1,0:T(8,128)(2,1)S(1)}, bf16[32,1024]{1,0:T(8,128)(2,1)S(1)}) custom-call(bf16[256,1024]{1,0:T(8,128)(2,1)} %refs_0_.1, bf16[1024,2048]{1,0:T(8,128)(2,1)} %refs_1_.3, bf16[256,1024]{1,0:T(8,128)(2,1)} %refs_2_.1), custom_call_target="tpu_custom_call" | custom-call | flops 268435456 | bytes 5242880 | tf_op jit(solution)/shard_map/pallas_call | solution.py:23
  1.9 0.0 copy-start
  1.9 3.1 %shard_map.56 = (bf16[256,512]{1,0:T(8,128)(2,1)S(1)}, bf16[256,512]{1,0:T(8,128)(2,1)S(1)}, bf16[256,256]{1,0:T(8,128)(2,1)S(1)}, bf16[256,256]{1,0:T(8,128)(2,1)S(1)}) custom-call(bf16[256,1024]{1,0:T(8,128)(2,1)S(1)} %get-tuple-element.40.refs_0_, bf16[1024,2048]{1,0:T(8,128)(2,1)} %refs_1_.3), custom_call_target="tpu_custom_call" | custom-call | flops 805306368 | bytes 4718592 | tf_op jit(solution)/shard_map/pallas_call | solution.py:23
  5.0 3.1 %collective-permute-start.2 = (bf16[320,512]{1,0:T(8,128)(2,1)S(1)}, bf16[320,512]{1,0:T(8,128)(2,1)S(1)}, u32[]{:S(2)}, u32[]{:S(2)}) collective-permute-start(bf16[320,512]{1,0:T(8,128)(2,1)S(1)} %shard_map.57), channel_id=1, source_target_pairs={{0,1},{1,0},{2,3},{3,2},{4,5},{5,4},{6,7},{7,6},{8,9},{9,8},{10,11... | collective-permute-start | bytes 983048 | tf_op jit(solution)/shard_map/ppermute | solution.py:42
  8.1 2.5 %collective-permute-start.1 = (bf16[320,512]{1,0:T(8,128)(2,1)S(1)}, bf16[320,512]{1,0:T(8,128)(2,1)S(1)}, u32[]{:S(2)}, u32[]{:S(2)}) collective-permute-start(bf16[320,512]{1,0:T(8,128)(2,1)S(1)} %get-tuple-element.42), channel_id=1, source_target_pairs={{0,3},{1,2},{2,1},{3,0},{4,7},{5,6},{6,5},{7,4},{8,11},{9,10},{10,... | collective-permute-start | bytes 983048 | tf_op jit(solution)/shard_map/ppermute | solution.py:42
  10.6 0.1 collective-permute-start.8
  10.7 17.3 %collective-permute-done.8.refs_2_ = bf16[32,1024]{1,0:T(8,128)(2,1)S(1)} collective-permute-done((bf16[32,1024]{1,0:T(8,128)(2,1)S(1)}, bf16[32,1024]{1,0:T(8,128)(2,1)S(1)}, u32[]{:S(2)}, u32[]{:S(2)}) %collective-permute-start.8) | collective-permute-done | bytes 65568 | tf_op jit(solution)/shard_map/ppermute | solution.py:42
  28.0 0.0 collective-permute-done.2.rest_0_.refs_1_
  28.0 0.0 collective-permute-done.1.rest_0_.refs_3_
  28.0 1.6 %collective-permute-start.9 = (bf16[4,32,1024]{2,1,0:T(8,128)(2,1)S(1)}, bf16[4,32,1024]{2,1,0:T(8,128)(2,1)S(1)}, u32[]{:S(2)}, u32[]{:S(2)}) collective-permute-start(bf16[4,32,1024]{2,1,0:T(8,128)(2,1)S(1)} %shard_map.64.refs_0_), channel_id=1, source_target_pairs={{0,8},{4,12},{8,0},{12,4},{1,9},{5,13},{9,1},{13,5},{2,10},{6,14},... | collective-permute-start | bytes 786440 | tf_op jit(solution)/shard_map/ppermute | solution.py:42
  29.5 1.0 %collective-permute-start.16 = (bf16[256,256]{1,0:T(8,128)(2,1)S(1)}, bf16[256,256]{1,0:T(8,128)(2,1)S(1)}, u32[]{:S(2)}, u32[]{:S(2)}) collective-permute-start(bf16[256,256]{1,0:T(8,128)(2,1)S(1)} %get-tuple-element.62), channel_id=1, source_target_pairs={{0,2},{1,3},{2,0},{3,1},{4,6},{5,7},{6,4},{7,5},{8,10},{9,11},{10,... | collective-permute-start | bytes 393224 | tf_op jit(solution)/shard_map/ppermute | solution.py:42
  30.6 1.9 %collective-permute-start = (bf16[256,256]{1,0:T(8,128)(2,1)S(1)}, bf16[256,256]{1,0:T(8,128)(2,1)S(1)}, u32[]{:S(2)}, u32[]{:S(2)}) collective-permute-start(bf16[256,256]{1,0:T(8,128)(2,1)S(1)} %get-tuple-element.41), channel_id=1, source_target_pairs={{0,2},{1,3},{2,0},{3,1},{4,6},{5,7},{6,4},{7,5},{8,10},{9,11},{10,... | collective-permute-start | bytes 393224 | tf_op jit(solution)/shard_map/ppermute | solution.py:42
  32.5 0.0 copy-done
  32.5 3.3 %shard_map.58 = (f32[4,64,2048]{2,1,0:T(8,128)S(1)}, f32[4,2,2048]{2,1,0:T(2,128)S(1)}) custom-call(bf16[4,64,2048]{2,1,0:T(8,128)(2,1)S(1)} %copy-done, bf16[256,512]{1,0:T(8,128)(2,1)S(1)} %get-tuple-element.45.rest_0_), custom_call_target="tpu_custom_call" | custom-call | flops 536870912 | bytes 1310720 | tf_op jit(solution)/shard_map/pallas_call | solution.py:23
  35.8 3.6 %shard_map.59 = (f32[4,64,2048]{2,1,0:T(8,128)S(1)}, f32[4,2,2048]{2,1,0:T(2,128)S(1)}) custom-call(bf16[4,64,2048]{2,1,0:T(8,128)(2,1)S(1)} %copy-done, bf16[320,512]{1,0:T(8,128)(2,1)S(1)} %collective-permute-done.2.rest_0_.refs_1_, f32[4,64,2048]{2,1,0:T(8,128)S(1)} %get-tuple-element.46.rest_1_, f32[4,2,2048]{2,1,0:T(2,128)S(1)} %get-tuple-element.47.rest_2_), custom_call_target="tpu_custom_call" | custom-call | flops 536870912 | bytes 3538944 | tf_op jit(solution)/shard_map/pallas_call | solution.py:23
  39.3 3.5 %shard_map.60 = (f32[4,64,2048]{2,1,0:T(8,128)S(1)}, f32[4,2,2048]{2,1,0:T(2,128)S(1)}) custom-call(bf16[4,64,2048]{2,1,0:T(8,128)(2,1)S(1)} %copy-done, bf16[320,512]{1,0:T(8,128)(2,1)S(1)} %collective-permute-done.1.rest_0_.refs_3_, f32[4,64,2048]{2,1,0:T(8,128)S(1)} %get-tuple-element.48.rest_1_, f32[4,2,2048]{2,1,0:T(2,128)S(1)} %get-tuple-element.49.rest_2_), custom_call_target="tpu_custom_call" | custom-call | flops 536870912 | bytes 3538944 | tf_op jit(solution)/shard_map/pallas_call | solution.py:23
  42.9 0.0 collective-permute-done.16.rest_0_
  42.9 2.2 %shard_map.66 = (bf16[2,72,1024]{2,1,0:T(8,128)(2,1)S(1)}, f32[2,64,1024]{2,1,0:T(8,128)S(1)}, f32[2,2,1024]{2,1,0:T(2,128)S(1)}) custom-call(bf16[4,64,2048]{2,1,0:T(8,128)(2,1)S(1)} %copy-done, bf16[256,256]{1,0:T(8,128)(2,1)S(1)} %collective-permute-done.16.rest_0_, f32[4,64,2048]{2,1,0:T(8,128)S(1)} %get-tuple-element.50.rest_1_, ...), custom_call_target="tpu_custom_call" | custom-call | flops 268435456 | bytes 3342336 | tf_op jit(solution)/shard_map/pallas_call | solution.py:23
  45.0 0.1 collective-permute-start.17
  45.1 0.0 collective-permute-done.rest_0_
  45.1 2.0 %shard_map.61 = (bf16[2,72,1024]{2,1,0:T(8,128)(2,1)S(1)}, f32[2,64,1024]{2,1,0:T(8,128)S(1)}, f32[2,2,1024]{2,1,0:T(2,128)S(1)}) custom-call(bf16[4,64,2048]{2,1,0:T(8,128)(2,1)S(1)} %copy-done, bf16[256,256]{1,0:T(8,128)(2,1)S(1)} %collective-permute-done.rest_0_, f32[4,64,2048]{2,1,0:T(8,128)S(1)} %get-tuple-element.50.rest_1_, ...), custom_call_target="tpu_custom_call" | custom-call | flops 268435456 | bytes 3342336 | tf_op jit(solution)/shard_map/pallas_call | solution.py:23
  47.1 0.6 collective-permute-start.3
  47.6 1.5 %collective-permute-start.10 = (bf16[4,32,1024]{2,1,0:T(8,128)(2,1)S(1)}, bf16[4,32,1024]{2,1,0:T(8,128)(2,1)S(1)}, u32[]{:S(2)}, u32[]{:S(2)}) collective-permute-start(bf16[4,32,1024]{2,1,0:T(8,128)(2,1)S(1)} %shard_map.64.refs_0_), channel_id=1, source_target_pairs={{0,16},{16,0},{1,17},{17,1},{2,18},{18,2},{3,19},{19,3},{4,20},{20... | collective-permute-start | bytes 786440 | tf_op jit(solution)/shard_map/ppermute | solution.py:42
  49.2 0.0 collective-permute-done.9.refs_1_
  49.2 0.5 collective-permute-start.11
  49.7 0.0 collective-permute-done.17.got_ref
  49.7 0.2 shard_map.67
  49.8 0.6 collective-permute-start.18
  50.4 0.0 collective-permute-start.12
  50.5 6.4 %collective-permute-done.10.refs_2_ = bf16[4,32,1024]{2,1,0:T(8,128)(2,1)S(1)} collective-permute-done((bf16[4,32,1024]{2,1,0:T(8,128)(2,1)S(1)}, bf16[4,32,1024]{2,1,0:T(8,128)(2,1)S(1)}, u32[]{:S(2)}, u32[]{:S(2)}) %collective-permute-start.10) | collective-permute-done | bytes 262176 | tf_op jit(solution)/shard_map/ppermute | solution.py:42
  56.8 0.0 collective-permute-start.13
  56.8 0.0 collective-permute-done.3.got_ref
  56.8 0.5 collective-permute-start.14
  57.3 4.2 %collective-permute-done.11.refs_3_ = bf16[4,32,1024]{2,1,0:T(8,128)(2,1)S(1)} collective-permute-done((bf16[4,32,1024]{2,1,0:T(8,128)(2,1)S(1)}, bf16[4,32,1024]{2,1,0:T(8,128)(2,1)S(1)}, u32[]{:S(2)}, u32[]{:S(2)}) %collective-permute-start.11) | collective-permute-done | bytes 262176 | tf_op jit(solution)/shard_map/ppermute | solution.py:42
  61.6 0.0 collective-permute-start.15
  61.6 0.2 shard_map.62
  61.7 0.0 collective-permute-done.18.got_ref
  61.7 0.6 collective-permute-start.4
  62.3 0.1 shard_map.68
  62.4 0.0 collective-permute-done.12.refs_4_
  62.4 0.4 collective-permute-start.19
  62.8 5.3 %collective-permute-done.4.got_ref = bf16[2,72,512]{2,1,0:T(8,128)(2,1)S(1)} collective-permute-done((bf16[2,72,512]{2,1,0:T(8,128)(2,1)S(1)}, bf16[2,72,512]{2,1,0:T(8,128)(2,1)S(1)}, u32[]{:S(2)}, u32[]{:S(2)}) %collective-permute-start.4) | collective-permute-done | bytes 147488 | tf_op jit(solution)/shard_map/ppermute | solution.py:42
  68.1 1.0 %collective-permute-start.20 = (bf16[2,64,128]{2,1,0:T(8,128)(2,1)S(1)}, bf16[2,64,128]{2,1,0:T(8,128)(2,1)S(1)}, u32[]{:S(2)}, u32[]{:S(2)}) collective-permute-start(bf16[2,64,128]{2,1,0:T(8,128)(2,1)S(1)} %get-tuple-element.71), channel_id=1, source_target_pairs={{0,2},{1,3},{2,0},{3,1},{4,6},{5,7},{6,4},{7,5},{8,10},{9,11},{10,... | collective-permute-start | bytes 98312 | tf_op jit(solution)/shard_map/ppermute | solution.py:42
  69.1 0.0 collective-permute-done.19.refs_1_
  69.1 1.6 %collective-permute-start.21 = (bf16[2,64,128]{2,1,0:T(8,128)(2,1)S(1)}, bf16[2,64,128]{2,1,0:T(8,128)(2,1)S(1)}, u32[]{:S(2)}, u32[]{:S(2)}) collective-permute-start(bf16[2,64,128]{2,1,0:T(8,128)(2,1)S(1)} %get-tuple-element.72), channel_id=1, source_target_pairs={{0,3},{1,2},{2,1},{3,0},{4,7},{5,6},{6,5},{7,4},{8,11},{9,10},{10,... | collective-permute-start | bytes 98312 | tf_op jit(solution)/shard_map/ppermute | solution.py:42
  70.7 0.1 shard_map.63
  70.8 0.0 collective-permute-done.13.refs_5_
  70.8 0.9 %collective-permute-start.5 = (bf16[2,64,128]{2,1,0:T(8,128)(2,1)S(1)}, bf16[2,64,128]{2,1,0:T(8,128)(2,1)S(1)}, u32[]{:S(2)}, u32[]{:S(2)}) collective-permute-start(bf16[2,64,128]{2,1,0:T(8,128)(2,1)S(1)} %get-tuple-element.59), channel_id=1, source_target_pairs={{0,1},{1,0},{2,3},{3,2},{4,5},{5,4},{6,7},{7,6},{8,9},{9,8},{10,11... | collective-permute-start | bytes 98312 | tf_op jit(solution)/shard_map/ppermute | solution.py:42
  71.7 0.0 collective-permute-done.14.refs_6_
  71.7 1.9 %collective-permute-start.6 = (bf16[2,64,128]{2,1,0:T(8,128)(2,1)S(1)}, bf16[2,64,128]{2,1,0:T(8,128)(2,1)S(1)}, u32[]{:S(2)}, u32[]{:S(2)}) collective-permute-start(bf16[2,64,128]{2,1,0:T(8,128)(2,1)S(1)} %get-tuple-element.60), channel_id=1, source_target_pairs={{0,2},{1,3},{2,0},{3,1},{4,6},{5,7},{6,4},{7,5},{8,10},{9,11},{10,... | collective-permute-start | bytes 98312 | tf_op jit(solution)/shard_map/ppermute | solution.py:42
  73.6 0.0 collective-permute-done.15.refs_7_
  73.7 0.0 copy-start.1
  73.7 1.6 %collective-permute-start.7 = (bf16[2,64,128]{2,1,0:T(8,128)(2,1)S(1)}, bf16[2,64,128]{2,1,0:T(8,128)(2,1)S(1)}, u32[]{:S(2)}, u32[]{:S(2)}) collective-permute-start(bf16[2,64,128]{2,1,0:T(8,128)(2,1)S(1)} %get-tuple-element.61), channel_id=1, source_target_pairs={{0,3},{1,2},{2,1},{3,0},{4,7},{5,6},{6,5},{7,4},{8,11},{9,10},{10,... | collective-permute-start | bytes 98312 | tf_op jit(solution)/shard_map/ppermute | solution.py:42
  75.3 0.2 shard_map.65.refs_5_
  75.4 0.0 collective-permute-done.20.refs_2_
  75.5 0.0 collective-permute-done.21.refs_3_
  75.5 0.0 copy-done.1
  75.5 0.5 shard_map.69
  76.0 0.0 collective-permute-done.5.refs_1_
  76.0 0.6 collective-permute-done.6.refs_2_
  76.5 2.8 %collective-permute-done.7.refs_3_ = bf16[2,64,128]{2,1,0:T(8,128)(2,1)S(1)} collective-permute-done((bf16[2,64,128]{2,1,0:T(8,128)(2,1)S(1)}, bf16[2,64,128]{2,1,0:T(8,128)(2,1)S(1)}, u32[]{:S(2)}, u32[]{:S(2)}) %collective-permute-start.7) | collective-permute-done | bytes 32800 | tf_op jit(solution)/shard_map/ppermute | solution.py:42
  79.4 1.2 %shard_map.70 = bf16[128,1024]{1,0:T(8,128)(2,1)} custom-call(bf16[2,64,128]{2,1,0:T(8,128)(2,1)S(1)} %get-tuple-element.58.refs_0_, bf16[2,64,128]{2,1,0:T(8,128)(2,1)S(1)} %collective-permute-done.5.refs_1_, bf16[2,64,128]{2,1,0:T(8,128)(2,1)S(1)} %collective-permute-done.6.refs_2_, bf16[2,64,128]{2,1,0:T(8,128)(2,1)S(1)} %collective-permute-done.7.refs_3_, ...), custom_call_target="tpu_custom_call" | custom-call | flops 134217728 | bytes 2757120 | tf_op jit(solution)/shard_map/pallas_call | solution.py:23
  (2 shorter events, 0.0 us)
Async XLA Ops:
  1.9 30.6 %copy-start = (bf16[4,64,2048]{2,1,0:T(8,128)(2,1)S(1)}, bf16[4,64,2048]{2,1,0:T(8,128)(2,1)}, u32[]{:S(2)}) copy-start(bf16[4,64,2048]{2,1,0:T(8,128)(2,1)} %q_ref.9) | copy-start | bytes 3145732
  5.0 23.0 %collective-permute-start.2 = (bf16[320,512]{1,0:T(8,128)(2,1)S(1)}, bf16[320,512]{1,0:T(8,128)(2,1)S(1)}, u32[]{:S(2)}, u32[]{:S(2)}) collective-permute-start(bf16[320,512]{1,0:T(8,128)(2,1)S(1)} %shard_map.57), channel_id=1, source_target_pairs={{0,1},{1,0},{2,3},{3,2},{4,5},{5,4},{6,7},{7,6},{8,9},{9,8},{10,11... | collective-permute-start | bytes 983048 | tf_op jit(solution)/shard_map/ppermute | solution.py:42
  8.1 19.9 %collective-permute-start.1 = (bf16[320,512]{1,0:T(8,128)(2,1)S(1)}, bf16[320,512]{1,0:T(8,128)(2,1)S(1)}, u32[]{:S(2)}, u32[]{:S(2)}) collective-permute-start(bf16[320,512]{1,0:T(8,128)(2,1)S(1)} %get-tuple-element.42), channel_id=1, source_target_pairs={{0,3},{1,2},{2,1},{3,0},{4,7},{5,6},{6,5},{7,4},{8,11},{9,10},{10,... | collective-permute-start | bytes 983048 | tf_op jit(solution)/shard_map/ppermute | solution.py:42
  10.6 17.4 %collective-permute-start.8 = (bf16[32,1024]{1,0:T(8,128)(2,1)S(1)}, bf16[32,1024]{1,0:T(8,128)(2,1)S(1)}, u32[]{:S(2)}, u32[]{:S(2)}) collective-permute-start(bf16[32,1024]{1,0:T(8,128)(2,1)S(1)} %get-tuple-element.44.own_ref.refs_0_), channel_id=1, source_target_pairs={{0,2},{1,3},{2,0},{3,1},{4,6},{5,7},{6,4},{7,5},{8,10},{9,11},{10,... | collective-permute-start | bytes 196616 | tf_op jit(solution)/shard_map/ppermute | solution.py:42
  28.0 21.2 %collective-permute-start.9 = (bf16[4,32,1024]{2,1,0:T(8,128)(2,1)S(1)}, bf16[4,32,1024]{2,1,0:T(8,128)(2,1)S(1)}, u32[]{:S(2)}, u32[]{:S(2)}) collective-permute-start(bf16[4,32,1024]{2,1,0:T(8,128)(2,1)S(1)} %shard_map.64.refs_0_), channel_id=1, source_target_pairs={{0,8},{4,12},{8,0},{12,4},{1,9},{5,13},{9,1},{13,5},{2,10},{6,14},... | collective-permute-start | bytes 786440 | tf_op jit(solution)/shard_map/ppermute | solution.py:42
  29.5 13.3 %collective-permute-start.16 = (bf16[256,256]{1,0:T(8,128)(2,1)S(1)}, bf16[256,256]{1,0:T(8,128)(2,1)S(1)}, u32[]{:S(2)}, u32[]{:S(2)}) collective-permute-start(bf16[256,256]{1,0:T(8,128)(2,1)S(1)} %get-tuple-element.62), channel_id=1, source_target_pairs={{0,2},{1,3},{2,0},{3,1},{4,6},{5,7},{6,4},{7,5},{8,10},{9,11},{10,... | collective-permute-start | bytes 393224 | tf_op jit(solution)/shard_map/ppermute | solution.py:42
  30.6 14.5 %collective-permute-start = (bf16[256,256]{1,0:T(8,128)(2,1)S(1)}, bf16[256,256]{1,0:T(8,128)(2,1)S(1)}, u32[]{:S(2)}, u32[]{:S(2)}) collective-permute-start(bf16[256,256]{1,0:T(8,128)(2,1)S(1)} %get-tuple-element.41), channel_id=1, source_target_pairs={{0,2},{1,3},{2,0},{3,1},{4,6},{5,7},{6,4},{7,5},{8,10},{9,11},{10,... | collective-permute-start | bytes 393224 | tf_op jit(solution)/shard_map/ppermute | solution.py:42
  45.0 4.7 %collective-permute-start.17 = (bf16[2,72,1024]{2,1,0:T(8,128)(2,1)S(1)}, bf16[2,72,1024]{2,1,0:T(8,128)(2,1)S(1)}, u32[]{:S(2)}, u32[]{:S(2)}) collective-permute-start(bf16[2,72,1024]{2,1,0:T(8,128)(2,1)S(1)} %get-tuple-element.63), channel_id=1, source_target_pairs={{0,4},{4,0},{8,12},{12,8},{1,5},{5,1},{9,13},{13,9},{2,6},{6,2},{1... | collective-permute-start | bytes 884744 | tf_op jit(solution)/shard_map/ppermute | solution.py:42
  47.1 9.7 %collective-permute-start.3 = (bf16[2,72,1024]{2,1,0:T(8,128)(2,1)S(1)}, bf16[2,72,1024]{2,1,0:T(8,128)(2,1)S(1)}, u32[]{:S(2)}, u32[]{:S(2)}) collective-permute-start(bf16[2,72,1024]{2,1,0:T(8,128)(2,1)S(1)} %get-tuple-element.52), channel_id=1, source_target_pairs={{0,4},{4,0},{8,12},{12,8},{1,5},{5,1},{9,13},{13,9},{2,6},{6,2},{1... | collective-permute-start | bytes 884744 | tf_op jit(solution)/shard_map/ppermute | solution.py:42
  47.6 9.2 %collective-permute-start.10 = (bf16[4,32,1024]{2,1,0:T(8,128)(2,1)S(1)}, bf16[4,32,1024]{2,1,0:T(8,128)(2,1)S(1)}, u32[]{:S(2)}, u32[]{:S(2)}) collective-permute-start(bf16[4,32,1024]{2,1,0:T(8,128)(2,1)S(1)} %shard_map.64.refs_0_), channel_id=1, source_target_pairs={{0,16},{16,0},{1,17},{17,1},{2,18},{18,2},{3,19},{19,3},{4,20},{20... | collective-permute-start | bytes 786440 | tf_op jit(solution)/shard_map/ppermute | solution.py:42
  49.2 12.4 %collective-permute-start.11 = (bf16[4,32,1024]{2,1,0:T(8,128)(2,1)S(1)}, bf16[4,32,1024]{2,1,0:T(8,128)(2,1)S(1)}, u32[]{:S(2)}, u32[]{:S(2)}) collective-permute-start(bf16[4,32,1024]{2,1,0:T(8,128)(2,1)S(1)} %collective-permute-done.9.refs_1_), channel_id=1, source_target_pairs={{0,16},{16,0},{1,17},{17,1},{2,18},{18,2},{3,19},{19,3},{4,20},{20... | collective-permute-start | bytes 786440 | tf_op jit(solution)/shard_map/ppermute | solution.py:42
  49.8 11.9 %collective-permute-start.18 = (bf16[2,72,512]{2,1,0:T(8,128)(2,1)S(1)}, bf16[2,72,512]{2,1,0:T(8,128)(2,1)S(1)}, u32[]{:S(2)}, u32[]{:S(2)}) collective-permute-start(bf16[2,72,512]{2,1,0:T(8,128)(2,1)S(1)} %get-tuple-element.66), channel_id=1, source_target_pairs={{0,8},{4,12},{8,0},{12,4},{1,9},{5,13},{9,1},{13,5},{2,10},{6,14},... | collective-permute-start | bytes 442376 | tf_op jit(solution)/shard_map/ppermute | solution.py:42
  50.4 12.0 %collective-permute-start.12 = (bf16[4,32,1024]{2,1,0:T(8,128)(2,1)S(1)}, bf16[4,32,1024]{2,1,0:T(8,128)(2,1)S(1)}, u32[]{:S(2)}, u32[]{:S(2)}) collective-permute-start(bf16[4,32,1024]{2,1,0:T(8,128)(2,1)S(1)} %shard_map.64.refs_0_), channel_id=1, source_target_pairs={{0,4},{4,0},{8,12},{12,8},{1,5},{5,1},{9,13},{13,9},{2,6},{6,2},{1... | collective-permute-start | bytes 786440 | tf_op jit(solution)/shard_map/ppermute | solution.py:42
  56.8 14.0 %collective-permute-start.13 = (bf16[4,32,1024]{2,1,0:T(8,128)(2,1)S(1)}, bf16[4,32,1024]{2,1,0:T(8,128)(2,1)S(1)}, u32[]{:S(2)}, u32[]{:S(2)}) collective-permute-start(bf16[4,32,1024]{2,1,0:T(8,128)(2,1)S(1)} %collective-permute-done.9.refs_1_), channel_id=1, source_target_pairs={{0,4},{4,0},{8,12},{12,8},{1,5},{5,1},{9,13},{13,9},{2,6},{6,2},{1... | collective-permute-start | bytes 786440 | tf_op jit(solution)/shard_map/ppermute | solution.py:42
  56.8 14.9 %collective-permute-start.14 = (bf16[4,32,1024]{2,1,0:T(8,128)(2,1)S(1)}, bf16[4,32,1024]{2,1,0:T(8,128)(2,1)S(1)}, u32[]{:S(2)}, u32[]{:S(2)}) collective-permute-start(bf16[4,32,1024]{2,1,0:T(8,128)(2,1)S(1)} %collective-permute-done.10.refs_2_), channel_id=1, source_target_pairs={{0,4},{4,0},{8,12},{12,8},{1,5},{5,1},{9,13},{13,9},{2,6},{6,2},{1... | collective-permute-start | bytes 786440 | tf_op jit(solution)/shard_map/ppermute | solution.py:42
  61.6 12.1 %collective-permute-start.15 = (bf16[4,32,1024]{2,1,0:T(8,128)(2,1)S(1)}, bf16[4,32,1024]{2,1,0:T(8,128)(2,1)S(1)}, u32[]{:S(2)}, u32[]{:S(2)}) collective-permute-start(bf16[4,32,1024]{2,1,0:T(8,128)(2,1)S(1)} %collective-permute-done.11.refs_3_), channel_id=1, source_target_pairs={{0,4},{4,0},{8,12},{12,8},{1,5},{5,1},{9,13},{13,9},{2,6},{6,2},{1... | collective-permute-start | bytes 786440 | tf_op jit(solution)/shard_map/ppermute | solution.py:42
  61.7 6.3 %collective-permute-start.4 = (bf16[2,72,512]{2,1,0:T(8,128)(2,1)S(1)}, bf16[2,72,512]{2,1,0:T(8,128)(2,1)S(1)}, u32[]{:S(2)}, u32[]{:S(2)}) collective-permute-start(bf16[2,72,512]{2,1,0:T(8,128)(2,1)S(1)} %get-tuple-element.55), channel_id=1, source_target_pairs={{0,8},{4,12},{8,0},{12,4},{1,9},{5,13},{9,1},{13,5},{2,10},{6,14},... | collective-permute-start | bytes 442376 | tf_op jit(solution)/shard_map/ppermute | solution.py:42
  62.4 6.7 %collective-permute-start.19 = (bf16[2,64,128]{2,1,0:T(8,128)(2,1)S(1)}, bf16[2,64,128]{2,1,0:T(8,128)(2,1)S(1)}, u32[]{:S(2)}, u32[]{:S(2)}) collective-permute-start(bf16[2,64,128]{2,1,0:T(8,128)(2,1)S(1)} %get-tuple-element.70), channel_id=1, source_target_pairs={{0,1},{1,0},{2,3},{3,2},{4,5},{5,4},{6,7},{7,6},{8,9},{9,8},{10,11... | collective-permute-start | bytes 98312 | tf_op jit(solution)/shard_map/ppermute | solution.py:42
  68.1 7.4 %collective-permute-start.20 = (bf16[2,64,128]{2,1,0:T(8,128)(2,1)S(1)}, bf16[2,64,128]{2,1,0:T(8,128)(2,1)S(1)}, u32[]{:S(2)}, u32[]{:S(2)}) collective-permute-start(bf16[2,64,128]{2,1,0:T(8,128)(2,1)S(1)} %get-tuple-element.71), channel_id=1, source_target_pairs={{0,2},{1,3},{2,0},{3,1},{4,6},{5,7},{6,4},{7,5},{8,10},{9,11},{10,... | collective-permute-start | bytes 98312 | tf_op jit(solution)/shard_map/ppermute | solution.py:42
  69.1 6.4 %collective-permute-start.21 = (bf16[2,64,128]{2,1,0:T(8,128)(2,1)S(1)}, bf16[2,64,128]{2,1,0:T(8,128)(2,1)S(1)}, u32[]{:S(2)}, u32[]{:S(2)}) collective-permute-start(bf16[2,64,128]{2,1,0:T(8,128)(2,1)S(1)} %get-tuple-element.72), channel_id=1, source_target_pairs={{0,3},{1,2},{2,1},{3,0},{4,7},{5,6},{6,5},{7,4},{8,11},{9,10},{10,... | collective-permute-start | bytes 98312 | tf_op jit(solution)/shard_map/ppermute | solution.py:42
  70.8 5.1 %collective-permute-start.5 = (bf16[2,64,128]{2,1,0:T(8,128)(2,1)S(1)}, bf16[2,64,128]{2,1,0:T(8,128)(2,1)S(1)}, u32[]{:S(2)}, u32[]{:S(2)}) collective-permute-start(bf16[2,64,128]{2,1,0:T(8,128)(2,1)S(1)} %get-tuple-element.59), channel_id=1, source_target_pairs={{0,1},{1,0},{2,3},{3,2},{4,5},{5,4},{6,7},{7,6},{8,9},{9,8},{10,11... | collective-permute-start | bytes 98312 | tf_op jit(solution)/shard_map/ppermute | solution.py:42
  71.7 4.8 %collective-permute-start.6 = (bf16[2,64,128]{2,1,0:T(8,128)(2,1)S(1)}, bf16[2,64,128]{2,1,0:T(8,128)(2,1)S(1)}, u32[]{:S(2)}, u32[]{:S(2)}) collective-permute-start(bf16[2,64,128]{2,1,0:T(8,128)(2,1)S(1)} %get-tuple-element.60), channel_id=1, source_target_pairs={{0,2},{1,3},{2,0},{3,1},{4,6},{5,7},{6,4},{7,5},{8,10},{9,11},{10,... | collective-permute-start | bytes 98312 | tf_op jit(solution)/shard_map/ppermute | solution.py:42
  73.7 1.8 %copy-start.1 = (f32[1024]{0:T(1024)S(1)}, f32[1024]{0:T(1024)}, u32[]{:S(2)}) copy-start(f32[1024]{0:T(1024)} %param.8) | copy-start | bytes 12292
  73.7 5.7 %collective-permute-start.7 = (bf16[2,64,128]{2,1,0:T(8,128)(2,1)S(1)}, bf16[2,64,128]{2,1,0:T(8,128)(2,1)S(1)}, u32[]{:S(2)}, u32[]{:S(2)}) collective-permute-start(bf16[2,64,128]{2,1,0:T(8,128)(2,1)S(1)} %get-tuple-element.61), channel_id=1, source_target_pairs={{0,3},{1,2},{2,1},{3,0},{4,7},{5,6},{6,5},{7,4},{8,11},{9,10},{10,... | collective-permute-start | bytes 98312 | tf_op jit(solution)/shard_map/ppermute | solution.py:42
